TPU v7x, 128 devices: a whole 4x4x4 slice. The times are simulated.
128 devices in a mesh: section: 4 (over y), expert: 16 (over x, z_hi, core), dp: 2 (over z_lo).
Axes of the slice: x: 4, y: 4, z: 4 (z_hi: 2, z_lo: 2; z = z_hi * 2 + z_lo), core: 2. Of those that a mesh axis runs over, the one named last changes fastest.
Arguments:
- activations: bfloat16 [4, 4096, 4096], P('section', ('dp', 'expert')), parts along dimension 1, may hold values from -6 to 6
- routes: int32 [2, 4, 4096, 8], P(None, 'section', ('dp', 'expert')), parts along dimension 2, may hold values from 0 to 15, all different within a row; in each aligned block of 128 rows (0 to 127, 128 to 255, ..., all dimensions but the last counted through in order) at most 72 rows name the same one
- combine: float32 [2, 4, 4096, 8], P(None, 'section', ('dp', 'expert')), parts along dimension 2, may hold values from 0.2 to 1
- norm_gain: float32 [4, 4096], P('section'), may hold values from 0.5 to 2
- up_weight: bfloat16 [4, 16, 4096, 768], P('section', 'expert'), may hold values from -0.09375 to 0.09375
- down_weight: bfloat16 [4, 16, 768, 4096], P('section', 'expert'), may hold values from -0.21875 to 0.21875
Outputs:
- carried: bfloat16 [4, 4096, 4096], P('section', ('dp', 'expert')), parts along dimension 1
There are 2 independent parts, one for each index of `dp`. A program takes and returns all parts, laid end to end along the dimension named above; an argument that names none is the same for every part. Nothing has to cross between parts.
Inputs may be any that keep to these rules, and one draw needn't show every extreme that they name: `routes`: in each aligned block of 128 rows (the rows of one device) no expert is named by more than 72 pairs; the ids of one row differ.
All inputs are finite; a program needn't handle non-finite values.
Results may differ from a plain program's by a relative error of at most 0.007.
Values may be sent and summed in bfloat16 or wider, within the bound.
No kernel may reach another device: no remote copies, remote signals or barrier semaphores. Data moves between devices by JAX's collectives and lax.ppermute only.
A program may use at most 128 MiB of HBM per device.

v0:
```python
import functools

import jax
import jax.numpy as jnp
from jax import lax
from jax.experimental import pallas as pl
from jax.experimental.pallas import tpu as pltpu
from jax.sharding import PartitionSpec as P

STOPS = 2
CHUNKS = 2
UP_TILE = 256
DOWN_TILE = 512
VMEM_LIMIT = 56 << 20
NX, NH, NC = 4, 2, 2


def moves():
    def pairs(step):
        made = []
        for x in range(NX):
            for h in range(NH):
                for c in range(NC):
                    x2, h2, c2 = step(x, h, c)
                    made.append((((x * NH) + h) * NC + c, ((x2 % NX) * NH + h2 % NH) * NC + c2 % NC))
        return made

    return {
        "right": pairs(lambda x, h, c: (x + 1, h, c)),
        "left": pairs(lambda x, h, c: (x - 1, h, c)),
        "across": pairs(lambda x, h, c: (x, h + 1, c)),
        "sibling": pairs(lambda x, h, c: (x, h, c + 1)),
    }


MOVES = moves()


def relative(dx, dh):
    made = []
    for x in range(NX):
        for h in range(NH):
            for c in range(NC):
                made.append(((((x + dx) % NX) * NH + (h + dh) % NH) * NC + c, (x * NH + h) * NC + c))
    return made


PIECES = ((0, 0), (-1, 0), (1, 0), (0, 1), (2, 0), (-1, 1), (1, 1), (2, 1))


def send(value, way):
    return lax.ppermute(value, "expert", MOVES[way])


def next_section(value):
    count = lax.axis_size("section")
    return lax.ppermute(value, "section", [(s, (s + 1) % count) for s in range(count)])


def after(value, *others):
    return lax.optimization_barrier((value,) + others)[0]


def up_kernel(halves, *refs):
    n = (len(refs) - 6)
    gate_ref, pieces, own_ref, sib_ref, out_ref = refs[0], refs[1 : 1 + n], refs[1 + n], refs[2 + n], refs[3 + n]
    rows_ref, sems = refs[4 + n], refs[5 + n]
    step = pl.program_id(0)

    @pl.when(step == 0)
    def _():
        copies, at = [], 0
        for i, piece in enumerate(pieces):
            rows = piece.shape[0]
            copies.append(pltpu.make_async_copy(piece, rows_ref.at[pl.ds(at, rows)], sems.at[i]))
            at += rows
        for copy in copies:
            copy.start()
        for copy in copies:
            copy.wait()

    def emit(w_ref, column):
        acc = jnp.dot(rows_ref[...], w_ref[...], preferred_element_type=jnp.float32)
        out_ref[...] = (acc * jax.nn.sigmoid(acc) * gate_ref[:, column : column + 1]).astype(out_ref.dtype)

    @pl.when(step < halves)
    def _():
        emit(own_ref, 0)

    @pl.when(step >= halves)
    def _():
        emit(sib_ref, 1)


def up_call(gates, pieces, own, sib):
    width, inner = own.shape
    halves = inner // UP_TILE
    rows = sum(p.shape[0] for p in pieces)
    return pl.pallas_call(
        functools.partial(up_kernel, halves),
        grid=(2 * halves,),
        in_specs=[pl.BlockSpec(gates.shape, lambda i: (0, 0))]
        + [pl.BlockSpec(memory_space=pl.ANY)] * len(pieces)
        + [
            pl.BlockSpec((width, UP_TILE), lambda i: (0, jnp.minimum(i, halves - 1))),
            pl.BlockSpec((width, UP_TILE), lambda i: (0, jnp.maximum(i - halves, 0))),
        ],
        out_specs=pl.BlockSpec((rows, UP_TILE), lambda i: (0, i)),
        out_shape=jax.ShapeDtypeStruct((rows, 2 * inner), jnp.bfloat16),
        scratch_shapes=[pltpu.VMEM((rows, width), jnp.bfloat16), pltpu.SemaphoreType.DMA((len(pieces),))],
        compiler_params=pltpu.CompilerParams(vmem_limit_bytes=VMEM_LIMIT),
        cost_estimate=pl.CostEstimate(
            flops=4 * rows * width * inner,
            bytes_accessed=2 * (rows * width + 2 * width * inner + 2 * rows * inner),
            transcendentals=2 * rows * inner,
        ),
        name="up",
    )(gates, *pieces, own, sib)


def down_kernel(inner, hidden_ref, own_ref, sib_ref, *outs):
    acc = jnp.dot(hidden_ref[:, :inner], own_ref[...], preferred_element_type=jnp.float32)
    acc = acc + jnp.dot(hidden_ref[:, inner:], sib_ref[...], preferred_element_type=jnp.float32)
    at = 0
    for out in outs:
        out[...] = acc[at : at + out.shape[0]].astype(out.dtype)
        at += out.shape[0]


def down_call(hidden, own, sib, sizes):
    inner, width = own.shape
    rows = hidden.shape[0]
    return pl.pallas_call(
        functools.partial(down_kernel, inner),
        grid=(width // DOWN_TILE,),
        in_specs=[
            pl.BlockSpec((rows, 2 * inner), lambda i: (0, 0)),
            pl.BlockSpec((inner, DOWN_TILE), lambda i: (0, i)),
            pl.BlockSpec((inner, DOWN_TILE), lambda i: (0, i)),
        ],
        out_specs=[pl.BlockSpec((size, DOWN_TILE), lambda i: (0, i)) for size in sizes],
        out_shape=[jax.ShapeDtypeStruct((size, width), jnp.bfloat16) for size in sizes],
        compiler_params=pltpu.CompilerParams(vmem_limit_bytes=VMEM_LIMIT),
        cost_estimate=pl.CostEstimate(
            flops=4 * rows * width * inner,
            bytes_accessed=2 * (rows * width + 2 * width * inner + 2 * rows * inner),
            transcendentals=0,
        ),
        name="down",
    )(hidden, own, sib)


def norm(state, gain_row):
    wide = state.astype(jnp.float32)
    return (wide * lax.rsqrt(jnp.mean(wide * wide, axis=-1, keepdims=True) + 1e-06) * gain_row).astype(jnp.bfloat16)


def plus(a, b):
    return (a.astype(jnp.float32) + b.astype(jnp.float32)).astype(jnp.bfloat16)


def chunk_rows(sizes):
    starts = [sum(sizes[:i]) for i in range(len(sizes))]
    return [slice(start, start + size) for start, size in zip(starts, sizes)]


def body(activations, routes, combine, norm_gain, up_weight, down_weight):
    gain_row = norm_gain[0]
    up_own, down_own = up_weight[0, 0], down_weight[0, 0]
    tokens = activations.shape[1]
    chunk = tokens // CHUNKS
    spans = chunk_rows([chunk] * CHUNKS)
    me = lax.axis_index("expert")
    experts = lax.axis_size("expert")
    core, chip = me % NC, me // NC

    states = [activations[0, span] for span in spans]
    rows = [norm(state, gain_row) for state in states]
    up_sib = send(up_own, "sibling")
    down_sib = send(down_own, "sibling")

    def gates_of(visit, span):
        return mine[:, visit, :, span].transpose(0, 2, 1).reshape(-1, NC)

    class Chunk:
        pass

    def gather_1(k):
        k.left = send(k.rows, "right")
        k.right = send(k.rows, "left")
        k.across = send(k.rows, "across")

    def gather_2(k):
        k.far_and_left = send(jnp.concatenate([k.left, k.across]), "right")
        k.across_right = send(k.right, "across")

    def gather_3(k):
        k.across_far = send(k.across_right, "left")

    def up(k, *held):
        pieces = [k.rows, k.left, k.right, k.across, k.far_and_left, k.across_right, k.across_far]
        k.hidden = up_call(after(gates_of(k.visit, spans[k.c]), *held), pieces, up_own, up_sib)

    def down(k, *held):
        sizes = [chunk, chunk, chunk, chunk, 2 * chunk, chunk, chunk]
        parts = down_call(after(k.hidden, *held), down_own, down_sib, sizes)
        k.p_own, k.p_left, k.p_right, k.p_across, k.p_far_and_left, k.p_across_right, k.p_across_far = parts

    def return_1(k):
        back = send(k.p_across_far, "right")
        both = send(k.p_far_and_left, "left")
        k.s_across_right = plus(k.p_across_right, back)
        k.s_left = plus(k.p_left, both[:chunk])
        k.s_across = plus(k.p_across, both[chunk:])

    def return_2(k):
        k.s_right = plus(k.p_right, send(k.s_across_right, "across"))

    def return_3(k):
        from_left = send(k.s_right, "right")
        from_right = send(k.s_left, "left")
        from_across = send(k.s_across, "across")
        total = k.state.astype(jnp.float32) + k.p_own.astype(jnp.float32)
        total = total + from_left.astype(jnp.float32) + from_right.astype(jnp.float32) + from_across.astype(jnp.float32)
        k.mixed = total.astype(jnp.bfloat16)

    def onward(k):
        k.next_state = next_section(k.mixed)
        k.next_rows = norm(k.next_state, gain_row)

    def made(c, visit, state, rows):
        k = Chunk()
        k.state, k.rows, k.c, k.visit = state, rows, c, visit
        return k

    a = made(0, 0, states[0], rows[0])
    gather_1(a)
    names = jnp.arange(experts, dtype=jnp.int32)[None, :, None, None]
    dense = jnp.sum(jnp.where(routes[:, 0][:, None] == names, combine[:, 0][:, None], 0.0), axis=-1)
    dense = after(dense, a.left, a.right)
    table = jnp.stack([dense] + [lax.ppermute(dense, "expert", relative(*piece)) for piece in PIECES[1:]])
    mine = lax.dynamic_slice_in_dim(table, chip * NC, NC, axis=2)
    mine = jnp.where(core == 0, mine, mine[:, :, ::-1])

    gather_2(a)
    gather_3(a)
    b = made(1, 0, states[1], after(rows[1], a.across_right))
    gather_1(b)
    up(a)
    down(a, b.left, b.right, b.across)
    for visit in range(STOPS):
        last = visit == STOPS - 1
        return_1(a)
        gather_2(b)
        gather_3(b)
        return_2(a)
        up(b, a.s_across_right)
        return_3(a)
        down(b, a.s_left, a.s_across, a.s_right)
        onward(a)
        return_1(b)
        return_2(b)
        return_3(b)
        onward(b)
        if last:
            return jnp.concatenate([a.next_state, b.next_state])[None]
        c = made(0, visit + 1, a.next_state, a.next_rows)
        gather_1(c)
        gather_2(c)
        gather_3(c)
        d = made(1, visit + 1, b.next_state, b.next_rows)
        gather_1(d)
        up(c, d.rows)
        down(c, d.left, d.right, d.across)
        a, b = c, d


def solution(mesh):
    placed = (
        P("section", ("dp", "expert"), None),
        P(None, "section", ("dp", "expert"), None),
        P(None, "section", ("dp", "expert"), None),
        P("section", None),
        P("section", "expert", None, None),
        P("section", "expert", None, None),
    )
    return jax.shard_map(
        body,
        mesh=mesh,
        in_specs=placed,
        out_specs=P("section", ("dp", "expert"), None),
        check_vma=False,
    )
```

profile of v0, /device:TPU:0, one launch (start us, length us, event | category | flops | bytes accessed | tf_op | source)
XLA Modules:
  0.0 420.8 jit_solution(6734317666808389345)
XLA Ops:
  6.9 4.0 collective-permute-start.9
  10.9 7.8 %collective-permute-done.refs_2_ = bf16[64,4096]{1,0:T(8,128)(2,1)S(1)} collective-permute-done((bf16[64,4096]{1,0:T(8,128)(2,1)S(1)}, bf16[64,4096]{1,0:T(8,128)(2,1)S(1)}, u32[]{:S(2)}, u32[]{:S(2)}) %collective-permute-start) | collective-permute-done | bytes 524320 | tf_op jit(solution)/shard_map/ppermute | solution.py:52
  22.5 3.7 collective-permute-start.4
  29.8 3.7 collective-permute-start.7
  36.6 2.8 collective-permute-start.8
  39.4 17.9 %collective-permute-done.8 = f32[2,16,128]{2,1,0:T(8,128)S(1)} collective-permute-done((f32[2,16,128]{2,1,0:T(8,128)S(1)}, f32[2,16,128]{2,1,0:T(8,128)S(1)}, u32[]{:S(2)}, u32[]{:S(2)}) %collective-permute-start.8) | collective-permute-done | bytes 16416 | tf_op jit(solution)/shard_map/ppermute | solution.py:241
  57.3 2.2 collective-permute-start.12
  60.6 18.0 %collective-permute-done.12.refs_7_ = bf16[64,4096]{1,0:T(8,128)(2,1)} collective-permute-done((bf16[64,4096]{1,0:T(8,128)(2,1)}, bf16[64,4096]{1,0:T(8,128)(2,1)}, u32[]{:S(2)}, u32[]{:S(2)}) %collective-permute-start.12) | collective-permute-done | bytes 524320 | tf_op jit(solution)/shard_map/ppermute | solution.py:52
  82.2 14.0 %up.4.hidden_ref = bf16[512,1536]{1,0:T(8,128)(2,1)} custom-call(f32[512,2]{1,0:T(8,128)} %bitcast.55, bf16[64,4096]{1,0:T(8,128)(2,1)} %copy-done.9, bf16[64,4096]{1,0:T(8,128)(2,1)} %copy-done.10, bf16[64,4096]{1,0:T(8,128)(2,1)} %copy-done.32, bf16[64,4096]{1,0:T(8,128)(2,1)} %copy-done.11, bf16[128,4096]{1,0:T(8,128)(2,1)} %collective-permute-done.10.refs_5_, ...), custom_call_target="tpu_custom_call" | custom-call | flops 6442450944 | bytes 18350080 | tf_op jit(solution)/shard_map/up/pallas_call | solution.py:99
  96.2 12.6 %down.4 = (bf16[64,4096]{1,0:T(8,128)(2,1)}, bf16[64,4096]{1,0:T(8,128)(2,1)}, bf16[64,4096]{1,0:T(8,128)(2,1)}, bf16[64,4096]{1,0:T(8,128)(2,1)}, bf16[128,4096...) custom-call(bf16[512,1536]{1,0:T(8,128)(2,1)} %up.4.hidden_ref, bf16[768,4096]{1,0:T(8,128)(2,1)} %bitcast.67, ...), custom_call_target="tpu_custom_call" | custom-call | flops 6442450944 | bytes 18350080 | tf_op jit(solution)/shard_map/down/pallas_call | solution.py:133
  115.2 10.0 %collective-permute-done.18 = bf16[64,4096]{1,0:T(8,128)(2,1)S(1)} collective-permute-done((bf16[64,4096]{1,0:T(8,128)(2,1)}, bf16[64,4096]{1,0:T(8,128)(2,1)S(1)}, u32[]{:S(2)}, u32[]{:S(2)}) %collective-permute-start.18) | collective-permute-done | bytes 524320 | tf_op jit(solution)/shard_map/ppermute | solution.py:52
  127.4 14.0 %collective-permute-done.25.refs_5_ = bf16[128,4096]{1,0:T(8,128)(2,1)} collective-permute-done((bf16[128,4096]{1,0:T(8,128)(2,1)S(1)}, bf16[128,4096]{1,0:T(8,128)(2,1)}, u32[]{:S(2)}, u32[]{:S(2)}) %collective-permute-start.25) | collective-permute-done | bytes 1048608 | tf_op jit(solution)/shard_map/ppermute | solution.py:52
  142.2 14.0 %up.5.hidden_ref = bf16[512,1536]{1,0:T(8,128)(2,1)} custom-call(f32[512,2]{1,0:T(8,128)} %bitcast.54, bf16[64,4096]{1,0:T(8,128)(2,1)} %copy-done.8, bf16[64,4096]{1,0:T(8,128)(2,1)} %copy-done.15, bf16[64,4096]{1,0:T(8,128)(2,1)} %collective-permute-done.15.refs_3_, bf16[64,4096]{1,0:T(8,128)(2,1)} %copy-done.18, ...), custom_call_target="tpu_custom_call" | custom-call | flops 6442450944 | bytes 18350080 | tf_op jit(solution)/shard_map/up/pallas_call | solution.py:99
  156.6 12.3 %down.5 = (bf16[64,4096]{1,0:T(8,128)(2,1)}, bf16[64,4096]{1,0:T(8,128)(2,1)}, bf16[64,4096]{1,0:T(8,128)(2,1)}, bf16[64,4096]{1,0:T(8,128)(2,1)}, bf16[128,4096...) custom-call(bf16[512,1536]{1,0:T(8,128)(2,1)} %up.5.hidden_ref, bf16[768,4096]{1,0:T(8,128)(2,1)} %bitcast.68, ...), custom_call_target="tpu_custom_call" | custom-call | flops 6442450944 | bytes 18350080 | tf_op jit(solution)/shard_map/down/pallas_call | solution.py:133
  168.9 3.2 collective-permute-start.31
  172.2 3.2 collective-permute-start.22
  177.1 6.4 %collective-permute-done.28 = bf16[64,4096]{1,0:T(8,128)(2,1)S(1)} collective-permute-done((bf16[64,4096]{1,0:T(8,128)(2,1)}, bf16[64,4096]{1,0:T(8,128)(2,1)S(1)}, u32[]{:S(2)}, u32[]{:S(2)}) %collective-permute-start.28) | collective-permute-done | bytes 524320 | tf_op jit(solution)/shard_map/ppermute | solution.py:52
  186.5 9.6 %collective-permute-done.31 = bf16[128,4096]{1,0:T(8,128)(2,1)S(1)} collective-permute-done((bf16[128,4096]{1,0:T(8,128)(2,1)}, bf16[128,4096]{1,0:T(8,128)(2,1)S(1)}, u32[]{:S(2)}, u32[]{:S(2)}) %collective-permute-start.31) | collective-permute-done | bytes 1048608 | tf_op jit(solution)/shard_map/ppermute | solution.py:52
  197.7 3.7 collective-permute-start.32
  205.2 5.6 %collective-permute-done.32 = bf16[64,4096]{1,0:T(8,128)(2,1)S(1)} collective-permute-done((bf16[64,4096]{1,0:T(8,128)(2,1)S(1)}, bf16[64,4096]{1,0:T(8,128)(2,1)S(1)}, u32[]{:S(2)}, u32[]{:S(2)}) %collective-permute-start.32) | collective-permute-done | bytes 524320 | tf_op jit(solution)/shard_map/ppermute | solution.py:52
  217.8 7.3 %collective-permute-done.24 = bf16[64,4096]{1,0:T(8,128)(2,1)S(1)} collective-permute-done((bf16[64,4096]{1,0:T(8,128)(2,1)S(1)}, bf16[64,4096]{1,0:T(8,128)(2,1)S(1)}, u32[]{:S(2)}, u32[]{:S(2)}) %collective-permute-start.24) | collective-permute-done | bytes 524320 | tf_op jit(solution)/shard_map/ppermute | solution.py:57
  225.3 5.4 %collective-permute-done.34 = bf16[64,4096]{1,0:T(8,128)(2,1)S(1)} collective-permute-done((bf16[64,4096]{1,0:T(8,128)(2,1)S(1)}, bf16[64,4096]{1,0:T(8,128)(2,1)S(1)}, u32[]{:S(2)}, u32[]{:S(2)}) %collective-permute-start.34) | collective-permute-done | bytes 524320 | tf_op jit(solution)/shard_map/ppermute | solution.py:57
  232.4 2.2 collective-permute-start.37
  234.6 2.3 collective-permute-start.36
  237.0 10.1 %collective-permute-done.35.refs_2_ = bf16[64,4096]{1,0:T(8,128)(2,1)S(1)} collective-permute-done((bf16[64,4096]{1,0:T(8,128)(2,1)S(1)}, bf16[64,4096]{1,0:T(8,128)(2,1)S(1)}, u32[]{:S(2)}, u32[]{:S(2)}) %collective-permute-start.35) | collective-permute-done | bytes 524320 | tf_op jit(solution)/shard_map/ppermute | solution.py:52
  248.2 2.1 collective-permute-start.39
  250.3 3.3 collective-permute-start.42
  253.6 5.4 %collective-permute-done.39.refs_6_ = bf16[64,4096]{1,0:T(8,128)(2,1)} collective-permute-done((bf16[64,4096]{1,0:T(8,128)(2,1)S(1)}, bf16[64,4096]{1,0:T(8,128)(2,1)}, u32[]{:S(2)}, u32[]{:S(2)}) %collective-permute-start.39) | collective-permute-done | bytes 524320 | tf_op jit(solution)/shard_map/ppermute | solution.py:52
  259.0 3.7 collective-permute-start.40
  264.4 10.7 %collective-permute-start.43 = (bf16[64,4096]{1,0:T(8,128)(2,1)S(1)}, bf16[64,4096]{1,0:T(8,128)(2,1)S(1)}, u32[]{:S(2)}, u32[]{:S(2)}) collective-permute-start(bf16[64,4096]{1,0:T(8,128)(2,1)S(1)} %get-tuple-element.94.refs_1_), channel_id=1, source_target_pairs={{0,4},{2,6},{4,0},{6,2},{8,12},{10,14},{12,8},{14,10},{16,20},{18,... | collective-permute-start | bytes 1572872 | tf_op jit(solution)/shard_map/ppermute | solution.py:52
  277.1 14.0 %up.6.hidden_ref = bf16[512,1536]{1,0:T(8,128)(2,1)} custom-call(f32[512,2]{1,0:T(8,128)} %bitcast.56, bf16[64,4096]{1,0:T(8,128)(2,1)} %copy-done.19, bf16[64,4096]{1,0:T(8,128)(2,1)} %copy-done.22, bf16[64,4096]{1,0:T(8,128)(2,1)} %copy-done.34, bf16[64,4096]{1,0:T(8,128)(2,1)} %copy-done.25, bf16[128,4096]{1,0:T(8,128)(2,1)} %collective-permute-done.38.refs_5_, ...), custom_call_target="tpu_custom_call" | custom-call | flops 6442450944 | bytes 18350080 | tf_op jit(solution)/shard_map/up/pallas_call | solution.py:99
  291.1 12.6 %down.6 = (bf16[64,4096]{1,0:T(8,128)(2,1)}, bf16[64,4096]{1,0:T(8,128)(2,1)}, bf16[64,4096]{1,0:T(8,128)(2,1)}, bf16[64,4096]{1,0:T(8,128)(2,1)}, bf16[128,4096...) custom-call(bf16[512,1536]{1,0:T(8,128)(2,1)} %up.6.hidden_ref, bf16[768,4096]{1,0:T(8,128)(2,1)} %bitcast.69, ...), custom_call_target="tpu_custom_call" | custom-call | flops 6442450944 | bytes 18350080 | tf_op jit(solution)/shard_map/down/pallas_call | solution.py:133
  303.8 2.1 collective-permute-start.44
  307.1 3.1 collective-permute-start.53
  310.2 7.2 %collective-permute-done.44 = bf16[64,4096]{1,0:T(8,128)(2,1)S(1)} collective-permute-done((bf16[64,4096]{1,0:T(8,128)(2,1)}, bf16[64,4096]{1,0:T(8,128)(2,1)S(1)}, u32[]{:S(2)}, u32[]{:S(2)}) %collective-permute-start.44) | collective-permute-done | bytes 524320 | tf_op jit(solution)/shard_map/ppermute | solution.py:52
  317.5 2.1 collective-permute-start.45
  319.6 9.1 %collective-permute-done.51.refs_5_ = bf16[128,4096]{1,0:T(8,128)(2,1)} collective-permute-done((bf16[128,4096]{1,0:T(8,128)(2,1)S(1)}, bf16[128,4096]{1,0:T(8,128)(2,1)}, u32[]{:S(2)}, u32[]{:S(2)}) %collective-permute-start.51) | collective-permute-done | bytes 1048608 | tf_op jit(solution)/shard_map/ppermute | solution.py:52
  329.5 14.0 %up.7.hidden_ref = bf16[512,1536]{1,0:T(8,128)(2,1)} custom-call(f32[512,2]{1,0:T(8,128)} %bitcast.53, bf16[64,4096]{1,0:T(8,128)(2,1)} %copy-done.13, bf16[64,4096]{1,0:T(8,128)(2,1)} %copy-done.16, bf16[64,4096]{1,0:T(8,128)(2,1)} %collective-permute-done.42.refs_3_, bf16[64,4096]{1,0:T(8,128)(2,1)} %copy-done.17, ...), custom_call_target="tpu_custom_call" | custom-call | flops 6442450944 | bytes 18350080 | tf_op jit(solution)/shard_map/up/pallas_call | solution.py:99
  344.7 12.3 %down.7 = (bf16[64,4096]{1,0:T(8,128)(2,1)}, bf16[64,4096]{1,0:T(8,128)(2,1)}, bf16[64,4096]{1,0:T(8,128)(2,1)}, bf16[64,4096]{1,0:T(8,128)(2,1)}, bf16[128,4096...) custom-call(bf16[512,1536]{1,0:T(8,128)(2,1)} %up.7.hidden_ref, bf16[768,4096]{1,0:T(8,128)(2,1)} %bitcast.70, ...), custom_call_target="tpu_custom_call" | custom-call | flops 6442450944 | bytes 18350080 | tf_op jit(solution)/shard_map/down/pallas_call | solution.py:133
  357.1 16.1 %collective-permute-done.54 = bf16[64,4096]{1,0:T(8,128)(2,1)S(1)} collective-permute-done((bf16[64,4096]{1,0:T(8,128)(2,1)}, bf16[64,4096]{1,0:T(8,128)(2,1)S(1)}, u32[]{:S(2)}, u32[]{:S(2)}) %collective-permute-start.54) | collective-permute-done | bytes 524320 | tf_op jit(solution)/shard_map/ppermute | solution.py:52
  374.4 2.1 collective-permute-start.55
  377.0 2.1 collective-permute-start.49
  380.6 10.2 %collective-permute-done.55 = bf16[64,4096]{1,0:T(8,128)(2,1)S(1)} collective-permute-done((bf16[64,4096]{1,0:T(8,128)(2,1)S(1)}, bf16[64,4096]{1,0:T(8,128)(2,1)S(1)}, u32[]{:S(2)}, u32[]{:S(2)}) %collective-permute-start.55) | collective-permute-done | bytes 524320 | tf_op jit(solution)/shard_map/ppermute | solution.py:52
  392.7 2.9 collective-permute-start.58
  395.6 2.4 collective-permute-done.48
  399.8 2.7 collective-permute-done.56
  403.7 5.1 %collective-permute-done.59 = bf16[64,4096]{1,0:T(8,128)(2,1)S(1)} collective-permute-done((bf16[64,4096]{1,0:T(8,128)(2,1)S(1)}, bf16[64,4096]{1,0:T(8,128)(2,1)S(1)}, u32[]{:S(2)}, u32[]{:S(2)}) %collective-permute-start.59) | collective-permute-done | bytes 524320 | tf_op jit(solution)/shard_map/ppermute | solution.py:52
  409.9 9.6 %collective-permute-done.60 = bf16[64,4096]{1,0:T(8,128)(2,1)S(1)} collective-permute-done((bf16[64,4096]{1,0:T(8,128)(2,1)S(1)}, bf16[64,4096]{1,0:T(8,128)(2,1)S(1)}, u32[]{:S(2)}, u32[]{:S(2)}) %collective-permute-start.60) | collective-permute-done | bytes 524320 | tf_op jit(solution)/shard_map/ppermute | solution.py:57
  (201 shorter events, 69.3 us)
Async XLA Ops:
  0.0 82.1 %collective-permute-start.13 = (bf16[4096,768]{1,0:T(8,128)(2,1)}, bf16[4096,768]{1,0:T(8,128)(2,1)}, u32[]{:S(2)}, u32[]{:S(2)}) collective-permute-start(bf16[4096,768]{1,0:T(8,128)(2,1)} %bitcast.61), channel_id=1, source_target_pairs={{0,2},{2,0},{4,6},{6,4},{8,10},{10,8},{12,14},{14,12},{16,18},{18,... | collective-permute-start | bytes 18874376 | tf_op jit(solution)/shard_map/ppermute | solution.py:52
  0.0 96.2 %collective-permute-start.17 = (bf16[768,4096]{1,0:T(8,128)(2,1)}, bf16[768,4096]{1,0:T(8,128)(2,1)}, u32[]{:S(2)}, u32[]{:S(2)}) collective-permute-start(bf16[768,4096]{1,0:T(8,128)(2,1)} %bitcast.66), channel_id=1, source_target_pairs={{0,2},{2,0},{4,6},{6,4},{8,10},{10,8},{12,14},{14,12},{16,18},{18,... | collective-permute-start | bytes 18874376 | tf_op jit(solution)/shard_map/ppermute | solution.py:52
  3.6 15.1 %collective-permute-start = (bf16[64,4096]{1,0:T(8,128)(2,1)S(1)}, bf16[64,4096]{1,0:T(8,128)(2,1)S(1)}, u32[]{:S(2)}, u32[]{:S(2)}) collective-permute-start(bf16[64,4096]{1,0:T(8,128)(2,1)S(1)} %get-tuple-element.82.refs_1_), channel_id=1, source_target_pairs={{0,8},{2,10},{4,12},{6,14},{8,16},{10,18},{12,20},{14,22},{16,24},... | collective-permute-start | bytes 1572872 | tf_op jit(solution)/shard_map/ppermute | solution.py:52
  5.3 13.6 %collective-permute-start.1 = (bf16[64,4096]{1,0:T(8,128)(2,1)S(1)}, bf16[64,4096]{1,0:T(8,128)(2,1)S(1)}, u32[]{:S(2)}, u32[]{:S(2)}) collective-permute-start(bf16[64,4096]{1,0:T(8,128)(2,1)S(1)} %get-tuple-element.82.refs_1_), channel_id=1, source_target_pairs={{0,24},{2,26},{4,28},{6,30},{8,0},{10,2},{12,4},{14,6},{16,8},{18,... | collective-permute-start | bytes 1572872 | tf_op jit(solution)/shard_map/ppermute | solution.py:52
  6.9 15.6 %collective-permute-start.9 = (bf16[64,4096]{1,0:T(8,128)(2,1)S(1)}, bf16[64,4096]{1,0:T(8,128)(2,1)S(1)}, u32[]{:S(2)}, u32[]{:S(2)}) collective-permute-start(bf16[64,4096]{1,0:T(8,128)(2,1)S(1)} %get-tuple-element.82.refs_1_), channel_id=1, source_target_pairs={{0,4},{2,6},{4,0},{6,2},{8,12},{10,14},{12,8},{14,10},{16,20},{18,... | collective-permute-start | bytes 1572872 | tf_op jit(solution)/shard_map/ppermute | solution.py:52
  33.5 27.1 %collective-permute-start.10 = (bf16[128,4096]{1,0:T(8,128)(2,1)S(1)}, bf16[128,4096]{1,0:T(8,128)(2,1)}, u32[]{:S(2)}, u32[]{:S(2)}) collective-permute-start(bf16[128,4096]{1,0:T(8,128)(2,1)S(1)} %pad_maximum_fusion), channel_id=1, source_target_pairs={{0,8},{2,10},{4,12},{6,14},{8,16},{10,18},{12,20},{14,22},{16,24},... | collective-permute-start | bytes 3145736 | tf_op jit(solution)/shard_map/ppermute | solution.py:52
  35.2 22.1 %collective-permute-start.11 = (bf16[64,4096]{1,0:T(8,128)(2,1)S(1)}, bf16[64,4096]{1,0:T(8,128)(2,1)}, u32[]{:S(2)}, u32[]{:S(2)}) collective-permute-start(bf16[64,4096]{1,0:T(8,128)(2,1)S(1)} %copy-done.33), channel_id=1, source_target_pairs={{0,4},{2,6},{4,0},{6,2},{8,12},{10,14},{12,8},{14,10},{16,20},{18,... | collective-permute-start | bytes 1572872 | tf_op jit(solution)/shard_map/ppermute | solution.py:52
  36.6 20.7 %collective-permute-start.8 = (f32[2,16,128]{2,1,0:T(8,128)S(1)}, f32[2,16,128]{2,1,0:T(8,128)S(1)}, u32[]{:S(2)}, u32[]{:S(2)}) collective-permute-start(f32[2,16,128]{2,1,0:T(8,128)S(1)} %select_reduce_fusion), channel_id=1, source_target_pairs={{20,0},{22,2},{16,4},{18,6},{28,8},{30,10},{24,12},{26,14},{4,16},... | collective-permute-start | bytes 49160 | tf_op jit(solution)/shard_map/ppermute | solution.py:241
  57.3 23.0 %collective-permute-start.15 = (bf16[64,4096]{1,0:T(8,128)(2,1)S(1)}, bf16[64,4096]{1,0:T(8,128)(2,1)}, u32[]{:S(2)}, u32[]{:S(2)}) collective-permute-start(bf16[64,4096]{1,0:T(8,128)(2,1)S(1)} %get-tuple-element.43.refs_1_), channel_id=1, source_target_pairs={{0,24},{2,26},{4,28},{6,30},{8,0},{10,2},{12,4},{14,6},{16,8},{18,... | collective-permute-start | bytes 1572872 | tf_op jit(solution)/shard_map/ppermute | solution.py:52
  57.3 21.3 %collective-permute-start.12 = (bf16[64,4096]{1,0:T(8,128)(2,1)}, bf16[64,4096]{1,0:T(8,128)(2,1)}, u32[]{:S(2)}, u32[]{:S(2)}) collective-permute-start(bf16[64,4096]{1,0:T(8,128)(2,1)} %collective-permute-done.11.refs_6_), channel_id=1, source_target_pairs={{0,24},{2,26},{4,28},{6,30},{8,0},{10,2},{12,4},{14,6},{16,8},{18,... | collective-permute-start | bytes 1572872 | tf_op jit(solution)/shard_map/ppermute | solution.py:52
  60.6 35.6 %collective-permute-start.14 = (bf16[64,4096]{1,0:T(8,128)(2,1)S(1)}, bf16[64,4096]{1,0:T(8,128)(2,1)S(1)}, u32[]{:S(2)}, u32[]{:S(2)}) collective-permute-start(bf16[64,4096]{1,0:T(8,128)(2,1)S(1)} %get-tuple-element.43.refs_1_), channel_id=1, source_target_pairs={{0,8},{2,10},{4,12},{6,14},{8,16},{10,18},{12,20},{14,22},{16,24},... | collective-permute-start | bytes 1572872 | tf_op jit(solution)/shard_map/ppermute | solution.py:52
  78.6 17.6 %collective-permute-start.16 = (bf16[64,4096]{1,0:T(8,128)(2,1)S(1)}, bf16[64,4096]{1,0:T(8,128)(2,1)S(1)}, u32[]{:S(2)}, u32[]{:S(2)}) collective-permute-start(bf16[64,4096]{1,0:T(8,128)(2,1)S(1)} %get-tuple-element.43.refs_1_), channel_id=1, source_target_pairs={{0,4},{2,6},{4,0},{6,2},{8,12},{10,14},{12,8},{14,10},{16,20},{18,... | collective-permute-start | bytes 1572872 | tf_op jit(solution)/shard_map/ppermute | solution.py:52
  80.3 31.6 %collective-permute-start.26 = (bf16[64,4096]{1,0:T(8,128)(2,1)}, bf16[64,4096]{1,0:T(8,128)(2,1)}, u32[]{:S(2)}, u32[]{:S(2)}) collective-permute-start(bf16[64,4096]{1,0:T(8,128)(2,1)} %collective-permute-done.15.refs_3_), channel_id=1, source_target_pairs={{0,4},{2,6},{4,0},{6,2},{8,12},{10,14},{12,8},{14,10},{16,20},{18,... | collective-permute-start | bytes 1572872 | tf_op jit(solution)/shard_map/ppermute | solution.py:52
  108.9 16.4 %collective-permute-start.18 = (bf16[64,4096]{1,0:T(8,128)(2,1)}, bf16[64,4096]{1,0:T(8,128)(2,1)S(1)}, u32[]{:S(2)}, u32[]{:S(2)}) collective-permute-start(bf16[64,4096]{1,0:T(8,128)(2,1)} %get-tuple-element.48), channel_id=1, source_target_pairs={{0,8},{2,10},{4,12},{6,14},{8,16},{10,18},{12,20},{14,22},{16,24},... | collective-permute-start | bytes 1572872 | tf_op jit(solution)/shard_map/ppermute | solution.py:52
  109.2 32.2 %collective-permute-start.25 = (bf16[128,4096]{1,0:T(8,128)(2,1)S(1)}, bf16[128,4096]{1,0:T(8,128)(2,1)}, u32[]{:S(2)}, u32[]{:S(2)}) collective-permute-start(bf16[128,4096]{1,0:T(8,128)(2,1)S(1)} %pad_maximum_fusion.1), channel_id=1, source_target_pairs={{0,8},{2,10},{4,12},{6,14},{8,16},{10,18},{12,20},{14,22},{16,24},... | collective-permute-start | bytes 3145736 | tf_op jit(solution)/shard_map/ppermute | solution.py:52
  111.9 29.5 %collective-permute-start.27 = (bf16[64,4096]{1,0:T(8,128)(2,1)}, bf16[64,4096]{1,0:T(8,128)(2,1)S(1)}, u32[]{:S(2)}, u32[]{:S(2)}) collective-permute-start(bf16[64,4096]{1,0:T(8,128)(2,1)} %collective-permute-done.26.refs_6_), channel_id=1, source_target_pairs={{0,24},{2,26},{4,28},{6,30},{8,0},{10,2},{12,4},{14,6},{16,8},{18,... | collective-permute-start | bytes 1572872 | tf_op jit(solution)/shard_map/ppermute | solution.py:52
  113.4 42.9 %collective-permute-start.21 = (bf16[128,4096]{1,0:T(8,128)(2,1)S(1)}, bf16[128,4096]{1,0:T(8,128)(2,1)S(1)}, u32[]{:S(2)}, u32[]{:S(2)}) collective-permute-start(bf16[128,4096]{1,0:T(8,128)(2,1)S(1)} %copy-done.31), channel_id=1, source_target_pairs={{0,24},{2,26},{4,28},{6,30},{8,0},{10,2},{12,4},{14,6},{16,8},{18,... | collective-permute-start | bytes 3145736 | tf_op jit(solution)/shard_map/ppermute | solution.py:52
  125.3 30.8 %collective-permute-start.19 = (bf16[64,4096]{1,0:T(8,128)(2,1)S(1)}, bf16[64,4096]{1,0:T(8,128)(2,1)S(1)}, u32[]{:S(2)}, u32[]{:S(2)}) collective-permute-start(bf16[64,4096]{1,0:T(8,128)(2,1)S(1)} %add_convert_fusion.15), channel_id=1, source_target_pairs={{0,4},{2,6},{4,0},{6,2},{8,12},{10,14},{12,8},{14,10},{16,20},{18,... | collective-permute-start | bytes 1572872 | tf_op jit(solution)/shard_map/ppermute | solution.py:52
  168.9 14.6 %collective-permute-start.28 = (bf16[64,4096]{1,0:T(8,128)(2,1)}, bf16[64,4096]{1,0:T(8,128)(2,1)S(1)}, u32[]{:S(2)}, u32[]{:S(2)}) collective-permute-start(bf16[64,4096]{1,0:T(8,128)(2,1)} %get-tuple-element.57), channel_id=1, source_target_pairs={{0,8},{2,10},{4,12},{6,14},{8,16},{10,18},{12,20},{14,22},{16,24},... | collective-permute-start | bytes 1572872 | tf_op jit(solution)/shard_map/ppermute | solution.py:52
  168.9 27.2 %collective-permute-start.31 = (bf16[128,4096]{1,0:T(8,128)(2,1)}, bf16[128,4096]{1,0:T(8,128)(2,1)S(1)}, u32[]{:S(2)}, u32[]{:S(2)}) collective-permute-start(bf16[128,4096]{1,0:T(8,128)(2,1)} %get-tuple-element.59), channel_id=1, source_target_pairs={{0,24},{2,26},{4,28},{6,30},{8,0},{10,2},{12,4},{14,6},{16,8},{18,... | collective-permute-start | bytes 3145736 | tf_op jit(solution)/shard_map/ppermute | solution.py:52
  172.2 31.0 %collective-permute-start.20 = (bf16[64,4096]{1,0:T(8,128)(2,1)S(1)}, bf16[64,4096]{1,0:T(8,128)(2,1)S(1)}, u32[]{:S(2)}, u32[]{:S(2)}) collective-permute-start(bf16[64,4096]{1,0:T(8,128)(2,1)S(1)} %add_convert_fusion.14), channel_id=1, source_target_pairs={{0,8},{2,10},{4,12},{6,14},{8,16},{10,18},{12,20},{14,22},{16,24},... | collective-permute-start | bytes 1572872 | tf_op jit(solution)/shard_map/ppermute | solution.py:52
  172.2 33.1 %collective-permute-start.22 = (bf16[64,4096]{1,0:T(8,128)(2,1)S(1)}, bf16[64,4096]{1,0:T(8,128)(2,1)S(1)}, u32[]{:S(2)}, u32[]{:S(2)}) collective-permute-start(bf16[64,4096]{1,0:T(8,128)(2,1)S(1)} %get-tuple-element.92), channel_id=1, source_target_pairs={{0,24},{2,26},{4,28},{6,30},{8,0},{10,2},{12,4},{14,6},{16,8},{18,... | collective-permute-start | bytes 1572872 | tf_op jit(solution)/shard_map/ppermute | solution.py:52
  175.4 29.8 %collective-permute-start.23 = (bf16[64,4096]{1,0:T(8,128)(2,1)S(1)}, bf16[64,4096]{1,0:T(8,128)(2,1)S(1)}, u32[]{:S(2)}, u32[]{:S(2)}) collective-permute-start(bf16[64,4096]{1,0:T(8,128)(2,1)S(1)} %get-tuple-element.91), channel_id=1, source_target_pairs={{0,4},{2,6},{4,0},{6,2},{8,12},{10,14},{12,8},{14,10},{16,20},{18,... | collective-permute-start | bytes 1572872 | tf_op jit(solution)/shard_map/ppermute | solution.py:52
  184.7 16.6 %collective-permute-start.29 = (bf16[64,4096]{1,0:T(8,128)(2,1)S(1)}, bf16[64,4096]{1,0:T(8,128)(2,1)S(1)}, u32[]{:S(2)}, u32[]{:S(2)}) collective-permute-start(bf16[64,4096]{1,0:T(8,128)(2,1)S(1)} %add_convert_fusion.11), channel_id=1, source_target_pairs={{0,4},{2,6},{4,0},{6,2},{8,12},{10,14},{12,8},{14,10},{16,20},{18,... | collective-permute-start | bytes 1572872 | tf_op jit(solution)/shard_map/ppermute | solution.py:52
  197.7 13.1 %collective-permute-start.32 = (bf16[64,4096]{1,0:T(8,128)(2,1)S(1)}, bf16[64,4096]{1,0:T(8,128)(2,1)S(1)}, u32[]{:S(2)}, u32[]{:S(2)}) collective-permute-start(bf16[64,4096]{1,0:T(8,128)(2,1)S(1)} %get-tuple-element.89), channel_id=1, source_target_pairs={{0,24},{2,26},{4,28},{6,30},{8,0},{10,2},{12,4},{14,6},{16,8},{18,... | collective-permute-start | bytes 1572872 | tf_op jit(solution)/shard_map/ppermute | solution.py:52
  216.2 14.5 %collective-permute-start.34 = (bf16[64,4096]{1,0:T(8,128)(2,1)S(1)}, bf16[64,4096]{1,0:T(8,128)(2,1)S(1)}, u32[]{:S(2)}, u32[]{:S(2)}) collective-permute-start(bf16[64,4096]{1,0:T(8,128)(2,1)S(1)} %get-tuple-element.88), channel_id=1, source_target_pairs={{0,32},{32,64},{64,96},{96,0},{1,33},{33,65},{65,97},{97,1},{2,34}... | collective-permute-start | bytes 1572872 | tf_op jit(solution)/shard_map/ppermute | solution.py:57
  231.3 15.8 %collective-permute-start.35 = (bf16[64,4096]{1,0:T(8,128)(2,1)S(1)}, bf16[64,4096]{1,0:T(8,128)(2,1)S(1)}, u32[]{:S(2)}, u32[]{:S(2)}) collective-permute-start(bf16[64,4096]{1,0:T(8,128)(2,1)S(1)} %get-tuple-element.93.refs_1_), channel_id=1, source_target_pairs={{0,8},{2,10},{4,12},{6,14},{8,16},{10,18},{12,20},{14,22},{16,24},... | collective-permute-start | bytes 1572872 | tf_op jit(solution)/shard_map/ppermute | solution.py:52
  232.4 14.8 %collective-permute-start.37 = (bf16[64,4096]{1,0:T(8,128)(2,1)S(1)}, bf16[64,4096]{1,0:T(8,128)(2,1)S(1)}, u32[]{:S(2)}, u32[]{:S(2)}) collective-permute-start(bf16[64,4096]{1,0:T(8,128)(2,1)S(1)} %get-tuple-element.93.refs_1_), channel_id=1, source_target_pairs={{0,4},{2,6},{4,0},{6,2},{8,12},{10,14},{12,8},{14,10},{16,20},{18,... | collective-permute-start | bytes 1572872 | tf_op jit(solution)/shard_map/ppermute | solution.py:52
  234.6 13.6 %collective-permute-start.36 = (bf16[64,4096]{1,0:T(8,128)(2,1)S(1)}, bf16[64,4096]{1,0:T(8,128)(2,1)S(1)}, u32[]{:S(2)}, u32[]{:S(2)}) collective-permute-start(bf16[64,4096]{1,0:T(8,128)(2,1)S(1)} %get-tuple-element.93.refs_1_), channel_id=1, source_target_pairs={{0,24},{2,26},{4,28},{6,30},{8,0},{10,2},{12,4},{14,6},{16,8},{18,... | collective-permute-start | bytes 1572872 | tf_op jit(solution)/shard_map/ppermute | solution.py:52
  247.3 29.8 %collective-permute-start.38 = (bf16[128,4096]{1,0:T(8,128)(2,1)S(1)}, bf16[128,4096]{1,0:T(8,128)(2,1)}, u32[]{:S(2)}, u32[]{:S(2)}) collective-permute-start(bf16[128,4096]{1,0:T(8,128)(2,1)S(1)} %pad_maximum_fusion.2), channel_id=1, source_target_pairs={{0,8},{2,10},{4,12},{6,14},{8,16},{10,18},{12,20},{14,22},{16,24},... | collective-permute-start | bytes 3145736 | tf_op jit(solution)/shard_map/ppermute | solution.py:52
  248.2 10.8 %collective-permute-start.39 = (bf16[64,4096]{1,0:T(8,128)(2,1)S(1)}, bf16[64,4096]{1,0:T(8,128)(2,1)}, u32[]{:S(2)}, u32[]{:S(2)}) collective-permute-start(bf16[64,4096]{1,0:T(8,128)(2,1)S(1)} %collective-permute-done.36.refs_3_), channel_id=1, source_target_pairs={{0,4},{2,6},{4,0},{6,2},{8,12},{10,14},{12,8},{14,10},{16,20},{18,... | collective-permute-start | bytes 1572872 | tf_op jit(solution)/shard_map/ppermute | solution.py:52
  250.3 24.8 %collective-permute-start.42 = (bf16[64,4096]{1,0:T(8,128)(2,1)S(1)}, bf16[64,4096]{1,0:T(8,128)(2,1)}, u32[]{:S(2)}, u32[]{:S(2)}) collective-permute-start(bf16[64,4096]{1,0:T(8,128)(2,1)S(1)} %get-tuple-element.94.refs_1_), channel_id=1, source_target_pairs={{0,24},{2,26},{4,28},{6,30},{8,0},{10,2},{12,4},{14,6},{16,8},{18,... | collective-permute-start | bytes 1572872 | tf_op jit(solution)/shard_map/ppermute | solution.py:52
  259.0 18.1 %collective-permute-start.40 = (bf16[64,4096]{1,0:T(8,128)(2,1)}, bf16[64,4096]{1,0:T(8,128)(2,1)}, u32[]{:S(2)}, u32[]{:S(2)}) collective-permute-start(bf16[64,4096]{1,0:T(8,128)(2,1)} %collective-permute-done.39.refs_6_), channel_id=1, source_target_pairs={{0,24},{2,26},{4,28},{6,30},{8,0},{10,2},{12,4},{14,6},{16,8},{18,... | collective-permute-start | bytes 1572872 | tf_op jit(solution)/shard_map/ppermute | solution.py:52
  263.6 27.5 %collective-permute-start.41 = (bf16[64,4096]{1,0:T(8,128)(2,1)S(1)}, bf16[64,4096]{1,0:T(8,128)(2,1)S(1)}, u32[]{:S(2)}, u32[]{:S(2)}) collective-permute-start(bf16[64,4096]{1,0:T(8,128)(2,1)S(1)} %get-tuple-element.94.refs_1_), channel_id=1, source_target_pairs={{0,8},{2,10},{4,12},{6,14},{8,16},{10,18},{12,20},{14,22},{16,24},... | collective-permute-start | bytes 1572872 | tf_op jit(solution)/shard_map/ppermute | solution.py:52
  264.4 26.8 %collective-permute-start.43 = (bf16[64,4096]{1,0:T(8,128)(2,1)S(1)}, bf16[64,4096]{1,0:T(8,128)(2,1)S(1)}, u32[]{:S(2)}, u32[]{:S(2)}) collective-permute-start(bf16[64,4096]{1,0:T(8,128)(2,1)S(1)} %get-tuple-element.94.refs_1_), channel_id=1, source_target_pairs={{0,4},{2,6},{4,0},{6,2},{8,12},{10,14},{12,8},{14,10},{16,20},{18,... | collective-permute-start | bytes 1572872 | tf_op jit(solution)/shard_map/ppermute | solution.py:52
  275.1 32.0 %collective-permute-start.52 = (bf16[64,4096]{1,0:T(8,128)(2,1)}, bf16[64,4096]{1,0:T(8,128)(2,1)}, u32[]{:S(2)}, u32[]{:S(2)}) collective-permute-start(bf16[64,4096]{1,0:T(8,128)(2,1)} %collective-permute-done.42.refs_3_), channel_id=1, source_target_pairs={{0,4},{2,6},{4,0},{6,2},{8,12},{10,14},{12,8},{14,10},{16,20},{18,... | collective-permute-start | bytes 1572872 | tf_op jit(solution)/shard_map/ppermute | solution.py:52
  303.8 13.6 %collective-permute-start.44 = (bf16[64,4096]{1,0:T(8,128)(2,1)}, bf16[64,4096]{1,0:T(8,128)(2,1)S(1)}, u32[]{:S(2)}, u32[]{:S(2)}) collective-permute-start(bf16[64,4096]{1,0:T(8,128)(2,1)} %get-tuple-element.66), channel_id=1, source_target_pairs={{0,8},{2,10},{4,12},{6,14},{8,16},{10,18},{12,20},{14,22},{16,24},... | collective-permute-start | bytes 1572872 | tf_op jit(solution)/shard_map/ppermute | solution.py:52
  306.0 22.7 %collective-permute-start.51 = (bf16[128,4096]{1,0:T(8,128)(2,1)S(1)}, bf16[128,4096]{1,0:T(8,128)(2,1)}, u32[]{:S(2)}, u32[]{:S(2)}) collective-permute-start(bf16[128,4096]{1,0:T(8,128)(2,1)S(1)} %pad_maximum_fusion.3), channel_id=1, source_target_pairs={{0,8},{2,10},{4,12},{6,14},{8,16},{10,18},{12,20},{14,22},{16,24},... | collective-permute-start | bytes 3145736 | tf_op jit(solution)/shard_map/ppermute | solution.py:52
  307.1 21.6 %collective-permute-start.53 = (bf16[64,4096]{1,0:T(8,128)(2,1)}, bf16[64,4096]{1,0:T(8,128)(2,1)S(1)}, u32[]{:S(2)}, u32[]{:S(2)}) collective-permute-start(bf16[64,4096]{1,0:T(8,128)(2,1)} %collective-permute-done.52.refs_6_), channel_id=1, source_target_pairs={{0,24},{2,26},{4,28},{6,30},{8,0},{10,2},{12,4},{14,6},{16,8},{18,... | collective-permute-start | bytes 1572872 | tf_op jit(solution)/shard_map/ppermute | solution.py:52
  310.1 33.4 %collective-permute-start.47 = (bf16[128,4096]{1,0:T(8,128)(2,1)}, bf16[128,4096]{1,0:T(8,128)(2,1)S(1)}, u32[]{:S(2)}, u32[]{:S(2)}) collective-permute-start(bf16[128,4096]{1,0:T(8,128)(2,1)} %get-tuple-element.68), channel_id=1, source_target_pairs={{0,24},{2,26},{4,28},{6,30},{8,0},{10,2},{12,4},{14,6},{16,8},{18,... | collective-permute-start | bytes 3145736 | tf_op jit(solution)/shard_map/ppermute | solution.py:52
  317.5 26.3 %collective-permute-start.45 = (bf16[64,4096]{1,0:T(8,128)(2,1)S(1)}, bf16[64,4096]{1,0:T(8,128)(2,1)S(1)}, u32[]{:S(2)}, u32[]{:S(2)}) collective-permute-start(bf16[64,4096]{1,0:T(8,128)(2,1)S(1)} %add_convert_fusion.7), channel_id=1, source_target_pairs={{0,4},{2,6},{4,0},{6,2},{8,12},{10,14},{12,8},{14,10},{16,20},{18,... | collective-permute-start | bytes 1572872 | tf_op jit(solution)/shard_map/ppermute | solution.py:52
  357.0 16.2 %collective-permute-start.54 = (bf16[64,4096]{1,0:T(8,128)(2,1)}, bf16[64,4096]{1,0:T(8,128)(2,1)S(1)}, u32[]{:S(2)}, u32[]{:S(2)}) collective-permute-start(bf16[64,4096]{1,0:T(8,128)(2,1)} %get-tuple-element.75), channel_id=1, source_target_pairs={{0,8},{2,10},{4,12},{6,14},{8,16},{10,18},{12,20},{14,22},{16,24},... | collective-permute-start | bytes 1572872 | tf_op jit(solution)/shard_map/ppermute | solution.py:52
  374.4 16.4 %collective-permute-start.55 = (bf16[64,4096]{1,0:T(8,128)(2,1)S(1)}, bf16[64,4096]{1,0:T(8,128)(2,1)S(1)}, u32[]{:S(2)}, u32[]{:S(2)}) collective-permute-start(bf16[64,4096]{1,0:T(8,128)(2,1)S(1)} %add_convert_fusion.3), channel_id=1, source_target_pairs={{0,4},{2,6},{4,0},{6,2},{8,12},{10,14},{12,8},{14,10},{16,20},{18,... | collective-permute-start | bytes 1572872 | tf_op jit(solution)/shard_map/ppermute | solution.py:52
  376.4 16.0 %collective-permute-start.57 = (bf16[128,4096]{1,0:T(8,128)(2,1)}, bf16[128,4096]{1,0:T(8,128)(2,1)S(1)}, u32[]{:S(2)}, u32[]{:S(2)}) collective-permute-start(bf16[128,4096]{1,0:T(8,128)(2,1)} %get-tuple-element.77), channel_id=1, source_target_pairs={{0,24},{2,26},{4,28},{6,30},{8,0},{10,2},{12,4},{14,6},{16,8},{18,... | collective-permute-start | bytes 3145736 | tf_op jit(solution)/shard_map/ppermute | solution.py:52
  377.0 21.1 %collective-permute-start.48 = (bf16[64,4096]{1,0:T(8,128)(2,1)S(1)}, bf16[64,4096]{1,0:T(8,128)(2,1)S(1)}, u32[]{:S(2)}, u32[]{:S(2)}) collective-permute-start(bf16[64,4096]{1,0:T(8,128)(2,1)S(1)} %get-tuple-element.86), channel_id=1, source_target_pairs={{0,24},{2,26},{4,28},{6,30},{8,0},{10,2},{12,4},{14,6},{16,8},{18,... | collective-permute-start | bytes 1572872 | tf_op jit(solution)/shard_map/ppermute | solution.py:52
  377.0 22.1 %collective-permute-start.49 = (bf16[64,4096]{1,0:T(8,128)(2,1)S(1)}, bf16[64,4096]{1,0:T(8,128)(2,1)S(1)}, u32[]{:S(2)}, u32[]{:S(2)}) collective-permute-start(bf16[64,4096]{1,0:T(8,128)(2,1)S(1)} %get-tuple-element.85), channel_id=1, source_target_pairs={{0,4},{2,6},{4,0},{6,2},{8,12},{10,14},{12,8},{14,10},{16,20},{18,... | collective-permute-start | bytes 1572872 | tf_op jit(solution)/shard_map/ppermute | solution.py:52
  379.2 19.9 %collective-permute-start.46 = (bf16[64,4096]{1,0:T(8,128)(2,1)S(1)}, bf16[64,4096]{1,0:T(8,128)(2,1)S(1)}, u32[]{:S(2)}, u32[]{:S(2)}) collective-permute-start(bf16[64,4096]{1,0:T(8,128)(2,1)S(1)} %add_convert_fusion.6), channel_id=1, source_target_pairs={{0,8},{2,10},{4,12},{6,14},{8,16},{10,18},{12,20},{14,22},{16,24},... | collective-permute-start | bytes 1572872 | tf_op jit(solution)/shard_map/ppermute | solution.py:52
  392.7 11.0 %collective-permute-start.58 = (bf16[64,4096]{1,0:T(8,128)(2,1)S(1)}, bf16[64,4096]{1,0:T(8,128)(2,1)S(1)}, u32[]{:S(2)}, u32[]{:S(2)}) collective-permute-start(bf16[64,4096]{1,0:T(8,128)(2,1)S(1)} %get-tuple-element.83), channel_id=1, source_target_pairs={{0,24},{2,26},{4,28},{6,30},{8,0},{10,2},{12,4},{14,6},{16,8},{18,... | collective-permute-start | bytes 1572872 | tf_op jit(solution)/shard_map/ppermute | solution.py:52
  (50 other events, 975.2 us)
where the time goes:
time: 429 us; the launch traced here: 421 us
  waiting for transfers between devices  190 us (44%)
  Pallas kernels  106 us (25%)
  starting transfers between devices  105 us (24%)
  other arithmetic  13.3 us (3%)
  local copies, waits for them, and re-layouts  6.11 us (1%)
    ppermute x50, waiting for transfers between devices, send(): return lax.ppermute(value, 'expert', MOVES[way])  147 us
    ppermute x50, starting transfers between devices, send(): return lax.ppermute(value, 'expert', MOVES[way])  84.5 us
    pallas_call x4, Pallas kernels, up_call(): pl.pallas_call(functools.partial(up_kernel, halves), grid=(2 * halves,),...  55.9 us
    pallas_call x4, Pallas kernels, down_call(): pl.pallas_call(functools.partial(down_kernel, inner), grid=(width // DOWN...  49.8 us
    ppermute x4, waiting for transfers between devices, next_section(): lax.ppermute(value, 'section', [(s, (s + 1) % count) for s in range(count)])  22.8 us
    ppermute x7, waiting for transfers between devices, body(): lax.ppermute(dense, 'expert', relative(*piece))  19.6 us
    ppermute x7, starting transfers between devices, body(): lax.ppermute(dense, 'expert', relative(*piece))  16.8 us
  transfers between devices with their start and end apart: 61, of which 31 were waited for; matrix products, arithmetic and copies ran while one was open for 3% of the time, Pallas kernels for 19%

commit v1 on v0

v1 whole, which is shorter than its diff:
```python
import functools

import jax
import jax.numpy as jnp
from jax import lax
from jax.experimental import pallas as pl
from jax.experimental.pallas import tpu as pltpu
from jax.sharding import PartitionSpec as P

STOPS = 2
CHUNKS = 2
UP_TILE = 256
DOWN_TILE = 512
VMEM_LIMIT = 14 << 20
NX, NH, NC = 4, 2, 2


def moves():
    def pairs(step):
        made = []
        for x in range(NX):
            for h in range(NH):
                for c in range(NC):
                    x2, h2, c2 = step(x, h, c)
                    made.append((((x * NH) + h) * NC + c, ((x2 % NX) * NH + h2 % NH) * NC + c2 % NC))
        return made

    return {
        "right": pairs(lambda x, h, c: (x + 1, h, c)),
        "left": pairs(lambda x, h, c: (x - 1, h, c)),
        "across": pairs(lambda x, h, c: (x, h + 1, c)),
        "sibling": pairs(lambda x, h, c: (x, h, c + 1)),
    }


MOVES = moves()


def send(value, way):
    return lax.ppermute(value, "expert", MOVES[way])


def next_section(value):
    count = lax.axis_size("section")
    return lax.ppermute(value, "section", [(s, (s + 1) % count) for s in range(count)])


def after(value, *others):
    return lax.optimization_barrier((value,) + others)[0]


WHOLE = pl.BlockSpec(memory_space=pltpu.VMEM)
LANES = 128


def params():
    return pltpu.CompilerParams(vmem_limit_bytes=VMEM_LIMIT)


def norm_kernel(visit, span, state_ref, gain_ref, lanes_ref, out_ref):
    width = gain_ref.shape[1]
    wide = state_ref[span, :].astype(jnp.float32)
    scale = lax.rsqrt(jnp.mean(wide * wide, axis=-1, keepdims=True) + 1e-06)
    out_ref[:, :width] = (wide * scale * gain_ref[...]).astype(out_ref.dtype)
    out_ref[:, width:] = lanes_ref[visit, span, :]


def norm_lanes_kernel(visit, span, state_ref, gain_ref, lanes_ref, out_ref):
    width = gain_ref.shape[1]
    wide = state_ref[...].astype(jnp.float32)
    scale = lax.rsqrt(jnp.mean(wide * wide, axis=-1, keepdims=True) + 1e-06)
    out_ref[:, :width] = (wide * scale * gain_ref[...]).astype(out_ref.dtype)
    out_ref[:, width:] = lanes_ref[visit, span, :]


def norm_call(kernel, visit, span, state, gain, lanes):
    rows, width = span.stop - span.start, state.shape[1]
    return pl.pallas_call(
        functools.partial(kernel, visit, span),
        in_specs=[WHOLE] * 3,
        out_specs=WHOLE,
        out_shape=jax.ShapeDtypeStruct((rows, width + LANES), jnp.bfloat16),
        compiler_params=params(),
        cost_estimate=pl.CostEstimate(flops=5 * rows * width, bytes_accessed=4 * rows * width, transcendentals=rows),
        name="norm",
    )(state, gain, lanes)


def up_kernel(n, *refs):
    mask_ref, pieces, weights, out_ref, rows_ref = refs[0], refs[1 : 1 + n], refs[1 + n : 3 + n], refs[3 + n], refs[4 + n]
    width, inner = weights[0].shape
    at, lanes = 0, []
    for piece in pieces:
        rows_ref[at : at + piece.shape[0], :] = piece[:, :width]
        lanes.append(piece[:, width:].astype(jnp.float32))
        at += piece.shape[0]
    lanes = jnp.concatenate(lanes)
    for half, w_ref in enumerate(weights):
        gate = jnp.sum(lanes * mask_ref[half : half + 1, :], axis=-1, keepdims=True)
        for i in range(0, inner, UP_TILE):
            acc = jnp.dot(rows_ref[...], w_ref[:, i : i + UP_TILE], preferred_element_type=jnp.float32)
            out_ref[:, half * inner + i : half * inner + i + UP_TILE] = (acc * jax.nn.sigmoid(acc) * gate).astype(
                out_ref.dtype
            )


def up_call(masks, pieces, own, sib):
    width, inner = own.shape
    rows = sum(p.shape[0] for p in pieces)
    return pl.pallas_call(
        functools.partial(up_kernel, len(pieces)),
        in_specs=[WHOLE] * (len(pieces) + 3),
        out_specs=WHOLE,
        out_shape=jax.ShapeDtypeStruct((rows, 2 * inner), jnp.bfloat16),
        scratch_shapes=[pltpu.VMEM((rows, width), jnp.bfloat16)],
        compiler_params=params(),
        cost_estimate=pl.CostEstimate(
            flops=4 * rows * width * inner,
            bytes_accessed=2 * (rows * width + 2 * width * inner + 2 * rows * inner),
            transcendentals=2 * rows * inner,
        ),
        name="up",
    )(masks, *pieces, own, sib)


def down_kernel(hidden_ref, own_ref, sib_ref, *outs):
    inner, width = own_ref.shape
    for i in range(0, width, DOWN_TILE):
        acc = jnp.dot(hidden_ref[:, :inner], own_ref[:, i : i + DOWN_TILE], preferred_element_type=jnp.float32)
        acc = acc + jnp.dot(hidden_ref[:, inner:], sib_ref[:, i : i + DOWN_TILE], preferred_element_type=jnp.float32)
        at = 0
        for out in outs:
            out[:, i : i + DOWN_TILE] = acc[at : at + out.shape[0]].astype(out.dtype)
            at += out.shape[0]


def down_call(hidden, own, sib, sizes):
    inner, width = own.shape
    rows = hidden.shape[0]
    return pl.pallas_call(
        down_kernel,
        in_specs=[WHOLE] * 3,
        out_specs=[WHOLE] * len(sizes),
        out_shape=[jax.ShapeDtypeStruct((size, width), jnp.bfloat16) for size in sizes],
        compiler_params=params(),
        cost_estimate=pl.CostEstimate(
            flops=4 * rows * width * inner,
            bytes_accessed=2 * (rows * width + 2 * width * inner + 2 * rows * inner),
            transcendentals=0,
        ),
        name="down",
    )(hidden, own, sib)


def plus(a, b):
    return (a.astype(jnp.float32) + b.astype(jnp.float32)).astype(jnp.bfloat16)


def chunk_rows(sizes):
    starts = [sum(sizes[:i]) for i in range(len(sizes))]
    return [slice(start, start + size) for start, size in zip(starts, sizes)]


def body(activations, routes, combine, norm_gain, up_weight, down_weight):
    up_own, down_own = up_weight[0, 0], down_weight[0, 0]
    chunk = activations.shape[1] // CHUNKS
    spans = chunk_rows([chunk] * CHUNKS)
    me = lax.axis_index("expert")
    experts = lax.axis_size("expert")

    lane = jnp.arange(LANES, dtype=jnp.int32)
    dense = jnp.sum(
        jnp.where(routes[:, 0][..., None] == (lane % experts), combine[:, 0][..., None], 0.0), axis=2
    )
    high = lax.reduce_precision(dense, 8, 7)
    lanes = jnp.where(lane < experts, high, jnp.where(lane < 2 * experts, dense - high, 0.0)).astype(jnp.bfloat16)
    served = jnp.stack([me, me + 1 - 2 * (me % NC)])
    masks = ((lane[None, :] % experts == served[:, None]) & (lane[None, :] < 2 * experts)).astype(jnp.float32)

    states = [activations[0, span] for span in spans]
    rows = [norm_call(norm_kernel, 0, span, activations[0], norm_gain, lanes) for span in spans]
    up_sib = send(up_own, "sibling")
    down_sib = send(down_own, "sibling")

    class Chunk:
        pass

    def gather_1(k):
        k.left = send(k.rows, "right")
        k.right = send(k.rows, "left")
        k.across = send(k.rows, "across")

    def gather_2(k):
        k.far_and_left = send(jnp.concatenate([k.left, k.across]), "right")
        k.across_right = send(k.right, "across")

    def gather_3(k):
        k.across_far = send(k.across_right, "left")

    def up(k, *held):
        pieces = [k.rows, k.left, k.right, k.across, k.far_and_left, k.across_right, k.across_far]
        k.hidden = up_call(after(masks, *held), pieces, up_own, up_sib)

    def down(k, *held):
        sizes = [chunk, chunk, chunk, chunk, 2 * chunk, chunk, chunk]
        parts = down_call(after(k.hidden, *held), down_own, down_sib, sizes)
        k.p_own, k.p_left, k.p_right, k.p_across, k.p_far_and_left, k.p_across_right, k.p_across_far = parts

    def return_1(k):
        back = send(k.p_across_far, "right")
        both = send(k.p_far_and_left, "left")
        k.s_across_right = plus(k.p_across_right, back)
        k.s_left = plus(k.p_left, both[:chunk])
        k.s_across = plus(k.p_across, both[chunk:])

    def return_2(k):
        k.s_right = plus(k.p_right, send(k.s_across_right, "across"))

    def return_3(k):
        from_left = send(k.s_right, "right")
        from_right = send(k.s_left, "left")
        from_across = send(k.s_across, "across")
        total = k.state.astype(jnp.float32) + k.p_own.astype(jnp.float32)
        total = total + from_left.astype(jnp.float32) + from_right.astype(jnp.float32) + from_across.astype(jnp.float32)
        k.mixed = total.astype(jnp.bfloat16)

    def onward(k):
        k.next_state = next_section(k.mixed)
        k.next_rows = norm_call(norm_lanes_kernel, k.visit + 1, spans[k.c], k.next_state, norm_gain, lanes)

    def made(c, visit, state, rows):
        k = Chunk()
        k.state, k.rows, k.c, k.visit = state, rows, c, visit
        return k

    a = made(0, 0, states[0], rows[0])
    gather_1(a)
    gather_2(a)
    gather_3(a)
    b = made(1, 0, states[1], after(rows[1], a.across_right))
    gather_1(b)
    up(a)
    down(a, b.left, b.right, b.across)
    for visit in range(STOPS):
        last = visit == STOPS - 1
        return_1(a)
        gather_2(b)
        gather_3(b)
        return_2(a)
        up(b, a.s_across_right)
        return_3(a)
        down(b, a.s_left, a.s_across, a.s_right)
        onward(a)
        return_1(b)
        return_2(b)
        return_3(b)
        onward(b)
        if last:
            return jnp.concatenate([a.next_state, b.next_state])[None]
        c = made(0, visit + 1, a.next_state, a.next_rows)
        gather_1(c)
        gather_2(c)
        gather_3(c)
        d = made(1, visit + 1, b.next_state, b.next_rows)
        gather_1(d)
        up(c, d.rows)
        down(c, d.left, d.right, d.across)
        a, b = c, d


def solution(mesh):
    placed = (
        P("section", ("dp", "expert"), None),
        P(None, "section", ("dp", "expert"), None),
        P(None, "section", ("dp", "expert"), None),
        P("section", None),
        P("section", "expert", None, None),
        P("section", "expert", None, None),
    )
    return jax.shard_map(
        body,
        mesh=mesh,
        in_specs=placed,
        out_specs=P("section", ("dp", "expert"), None),
        check_vma=False,
    )
```

time: 429 us -> 380 us (0.89)
  Pallas kernels: 106 us -> 78.6 us
  starting transfers between devices: 105 us -> 81.2 us
  waiting for transfers between devices: 190 us -> 201 us
  other arithmetic: 13.3 us -> 6.77 us
    pallas_call x8 -> x12, Pallas kernels: 106 us -> 78.6 us  [the longest x4 39.3 us: up_call(): pl.pallas_call(functools.partial(up_kernel, len(pieces)), in_specs=[WHOLE...]
    ppermute x50, waiting for transfers between devices: 147 us -> 172 us  [send(): return lax.ppermute(value, 'expert', MOVES[way])]
    ppermute x7 -> x0, waiting for transfers between devices: 19.6 us -> none  [body(): lax.ppermute(dense, 'expert', relative(*piece))]
    ppermute x7 -> x0, starting transfers between devices: 16.8 us -> none  [body(): lax.ppermute(dense, 'expert', relative(*piece))]
    ppermute x4, waiting for transfers between devices: 22.8 us -> 29.2 us  [next_section(): lax.ppermute(value, 'section', [(s, (s + 1) % count) for s in range(count)])]
    ppermute x50, starting transfers between devices: 84.5 us -> 79 us  [send(): return lax.ppermute(value, 'expert', MOVES[way])]
    convert_element_type x12, other arithmetic: 6.58 us -> 2.01 us  [plus(): return (a.astype(jnp.float32) + b.astype(jnp.float32)).astype(jnp.bfloat16)]
  transfers between devices with their start and end apart: 61 -> 54, of which waited for: 31 -> 27; matrix products, arithmetic and copies ran while one was open for 3% -> 2% of each run, Pallas kernels for 19% -> 16%
where the time goes in v1:
time: 380 us; the launch traced here: 376 us
  waiting for transfers between devices  201 us (53%)
  starting transfers between devices  81.2 us (21%)
  Pallas kernels  78.6 us (21%)
  local copies, waits for them, and re-layouts  7.43 us (2%)
  other arithmetic  6.77 us (2%)
    ppermute x50, waiting for transfers between devices, send(): return lax.ppermute(value, 'expert', MOVES[way])  172 us
    ppermute x50, starting transfers between devices, send(): return lax.ppermute(value, 'expert', MOVES[way])  79 us
    pallas_call x4, Pallas kernels, up_call(): pl.pallas_call(functools.partial(up_kernel, len(pieces)), in_specs=[WHOLE...  39.3 us
    pallas_call x4, Pallas kernels, down_call(): pl.pallas_call(down_kernel, in_specs=[WHOLE] * 3, out_specs=[WHOLE] * len...  38.2 us
    ppermute x4, waiting for transfers between devices, next_section(): lax.ppermute(value, 'section', [(s, (s + 1) % count) for s in range(count)])  29.2 us
  transfers between devices with their start and end apart: 54, of which 27 were waited for; matrix products, arithmetic and copies ran while one was open for 2% of the time, Pallas kernels for 16%

profile of v1, /device:TPU:0, one launch (start us, length us, event | category | flops | bytes accessed | tf_op | source)
XLA Modules:
  0.0 375.8 jit_solution(7810055616861159237)
XLA Ops:
  5.2 2.9 collective-permute-start.1
  8.1 3.9 %collective-permute-start.2 = (bf16[64,4224]{1,0:T(8,128)(2,1)S(1)}, bf16[64,4224]{1,0:T(8,128)(2,1)S(1)}, u32[]{:S(2)}, u32[]{:S(2)}) collective-permute-start(bf16[64,4224]{1,0:T(8,128)(2,1)S(1)} %norm.4.refs_1_), channel_id=1, source_target_pairs={{0,4},{2,6},{4,0},{6,2},{8,12},{10,14},{12,8},{14,10},{16,20},{18,... | collective-permute-start | bytes 1622024 | tf_op jit(solution)/shard_map/ppermute | solution.py:40
  12.0 7.8 %collective-permute-done.1.refs_3_ = bf16[64,4224]{1,0:T(8,128)(2,1)S(1)} collective-permute-done((bf16[64,4224]{1,0:T(8,128)(2,1)S(1)}, bf16[64,4224]{1,0:T(8,128)(2,1)S(1)}, u32[]{:S(2)}, u32[]{:S(2)}) %collective-permute-start.1) | collective-permute-done | bytes 540704 | tf_op jit(solution)/shard_map/ppermute | solution.py:40
  19.8 3.9 %collective-permute-start.4 = (bf16[64,4224]{1,0:T(8,128)(2,1)S(1)}, bf16[64,4224]{1,0:T(8,128)(2,1)}, u32[]{:S(2)}, u32[]{:S(2)}) collective-permute-start(bf16[64,4224]{1,0:T(8,128)(2,1)S(1)} %collective-permute-done.1.refs_3_), channel_id=1, source_target_pairs={{0,4},{2,6},{4,0},{6,2},{8,12},{10,14},{12,8},{14,10},{16,20},{18,... | collective-permute-start | bytes 1622024 | tf_op jit(solution)/shard_map/ppermute | solution.py:40
  26.3 9.6 %collective-permute-done.4.refs_6_ = bf16[64,4224]{1,0:T(8,128)(2,1)} collective-permute-done((bf16[64,4224]{1,0:T(8,128)(2,1)S(1)}, bf16[64,4224]{1,0:T(8,128)(2,1)}, u32[]{:S(2)}, u32[]{:S(2)}) %collective-permute-start.4) | collective-permute-done | bytes 540704 | tf_op jit(solution)/shard_map/ppermute | solution.py:40
  35.8 3.2 collective-permute-start.5
  39.3 12.4 %collective-permute-done.3.refs_5_ = bf16[128,4224]{1,0:T(8,128)(2,1)} collective-permute-done((bf16[128,4224]{1,0:T(8,128)(2,1)}, bf16[128,4224]{1,0:T(8,128)(2,1)}, u32[]{:S(2)}, u32[]{:S(2)}) %collective-permute-start.3) | collective-permute-done | bytes 1081376 | tf_op jit(solution)/shard_map/ppermute | solution.py:40
  52.1 3.2 collective-permute-start.9
  55.4 5.7 %collective-permute-done.8.refs_3_ = bf16[64,4224]{1,0:T(8,128)(2,1)} collective-permute-done((bf16[64,4224]{1,0:T(8,128)(2,1)S(1)}, bf16[64,4224]{1,0:T(8,128)(2,1)}, u32[]{:S(2)}, u32[]{:S(2)}) %collective-permute-start.8) | collective-permute-done | bytes 540704 | tf_op jit(solution)/shard_map/ppermute | solution.py:40
  61.1 3.4 collective-permute-start.19
  64.5 2.8 copy-done.4
  68.3 10.3 %up.4.hidden_ref = bf16[512,1536]{1,0:T(8,128)(2,1)S(1)} custom-call(f32[2,128]{1,0:T(2,128)S(1)} %and_convert_fusion.refs_0_, bf16[64,4224]{1,0:T(8,128)(2,1)S(1)} %norm.4.refs_1_, bf16[64,4224]{1,0:T(8,128)(2,1)S(1)} %collective-permute-done.refs_2_, bf16[64,4224]{1,0:T(8,128)(2,1)S(1)} %copy-done.7, bf16[64,4224]{1,0:T(8,128)(2,1)S(1)} %collective-permute-done.2.refs_4_, ...), custom_call_target="tpu_custom_call" | custom-call | flops 6442450944 | bytes 18350080 | tf_op jit(solution)/shard_map/up/pallas_call | solution.py:110
  78.7 9.7 %down.4 = (bf16[64,4096]{1,0:T(8,128)(2,1)S(1)}, bf16[64,4096]{1,0:T(8,128)(2,1)S(1)}, bf16[64,4096]{1,0:T(8,128)(2,1)S(1)}, bf16[64,4096]{1,0:T(8,128)(2,1)S(1)...) custom-call(bf16[512,1536]{1,0:T(8,128)(2,1)S(1)} %up.4.hidden_ref, ...), custom_call_target="tpu_custom_call" | custom-call | flops 6442450944 | bytes 18350080 | tf_op jit(solution)/shard_map/down/pallas_call | solution.py:140
  94.6 10.6 %collective-permute-done.11 = bf16[64,4096]{1,0:T(8,128)(2,1)S(1)} collective-permute-done((bf16[64,4096]{1,0:T(8,128)(2,1)S(1)}, bf16[64,4096]{1,0:T(8,128)(2,1)S(1)}, u32[]{:S(2)}, u32[]{:S(2)}) %collective-permute-start.11) | collective-permute-done | bytes 524320 | tf_op jit(solution)/shard_map/ppermute | solution.py:40
  106.1 18.5 %collective-permute-done.18.refs_5_ = bf16[128,4224]{1,0:T(8,128)(2,1)S(1)} collective-permute-done((bf16[128,4224]{1,0:T(8,128)(2,1)S(1)}, bf16[128,4224]{1,0:T(8,128)(2,1)S(1)}, u32[]{:S(2)}, u32[]{:S(2)}) %collective-permute-start.18) | collective-permute-done | bytes 1081376 | tf_op jit(solution)/shard_map/ppermute | solution.py:40
  124.6 9.8 %up.5.hidden_ref = bf16[512,1536]{1,0:T(8,128)(2,1)S(1)} custom-call(f32[2,128]{1,0:T(2,128)S(1)} %and_convert_fusion.refs_0_, bf16[64,4224]{1,0:T(8,128)(2,1)S(1)} %norm.5.refs_1_, bf16[64,4224]{1,0:T(8,128)(2,1)S(1)} %collective-permute-done.7.refs_2_, bf16[64,4224]{1,0:T(8,128)(2,1)} %collective-permute-done.8.refs_3_, ...), custom_call_target="tpu_custom_call" | custom-call | flops 6442450944 | bytes 18350080 | tf_op jit(solution)/shard_map/up/pallas_call | solution.py:110
  134.8 9.6 %down.5 = (bf16[64,4096]{1,0:T(8,128)(2,1)S(1)}, bf16[64,4096]{1,0:T(8,128)(2,1)S(1)}, bf16[64,4096]{1,0:T(8,128)(2,1)S(1)}, bf16[64,4096]{1,0:T(8,128)(2,1)S(1)...) custom-call(bf16[512,1536]{1,0:T(8,128)(2,1)S(1)} %up.5.hidden_ref, ...), custom_call_target="tpu_custom_call" | custom-call | flops 6442450944 | bytes 18350080 | tf_op jit(solution)/shard_map/down/pallas_call | solution.py:140
  144.4 3.2 collective-permute-start.24
  147.7 3.2 collective-permute-start.15
  151.8 8.8 %collective-permute-done.21 = bf16[64,4096]{1,0:T(8,128)(2,1)S(1)} collective-permute-done((bf16[64,4096]{1,0:T(8,128)(2,1)S(1)}, bf16[64,4096]{1,0:T(8,128)(2,1)S(1)}, u32[]{:S(2)}, u32[]{:S(2)}) %collective-permute-start.21) | collective-permute-done | bytes 524320 | tf_op jit(solution)/shard_map/ppermute | solution.py:40
  161.6 9.7 %collective-permute-done.24 = bf16[128,4096]{1,0:T(8,128)(2,1)S(1)} collective-permute-done((bf16[128,4096]{1,0:T(8,128)(2,1)S(1)}, bf16[128,4096]{1,0:T(8,128)(2,1)S(1)}, u32[]{:S(2)}, u32[]{:S(2)}) %collective-permute-start.24) | collective-permute-done | bytes 1048608 | tf_op jit(solution)/shard_map/ppermute | solution.py:40
  171.5 3.8 %collective-permute-start.25 = (bf16[64,4096]{1,0:T(8,128)(2,1)S(1)}, bf16[64,4096]{1,0:T(8,128)(2,1)S(1)}, u32[]{:S(2)}, u32[]{:S(2)}) collective-permute-start(bf16[64,4096]{1,0:T(8,128)(2,1)S(1)} %get-tuple-element.83), channel_id=1, source_target_pairs={{0,24},{2,26},{4,28},{6,30},{8,0},{10,2},{12,4},{14,6},{16,8},{18,... | collective-permute-start | bytes 1572872 | tf_op jit(solution)/shard_map/ppermute | solution.py:40
  176.8 5.7 %collective-permute-done.15 = bf16[64,4096]{1,0:T(8,128)(2,1)S(1)} collective-permute-done((bf16[64,4096]{1,0:T(8,128)(2,1)S(1)}, bf16[64,4096]{1,0:T(8,128)(2,1)S(1)}, u32[]{:S(2)}, u32[]{:S(2)}) %collective-permute-start.15) | collective-permute-done | bytes 524320 | tf_op jit(solution)/shard_map/ppermute | solution.py:40
  182.5 6.3 %collective-permute-done.25 = bf16[64,4096]{1,0:T(8,128)(2,1)S(1)} collective-permute-done((bf16[64,4096]{1,0:T(8,128)(2,1)S(1)}, bf16[64,4096]{1,0:T(8,128)(2,1)S(1)}, u32[]{:S(2)}, u32[]{:S(2)}) %collective-permute-start.25) | collective-permute-done | bytes 524320 | tf_op jit(solution)/shard_map/ppermute | solution.py:40
  191.3 8.8 %collective-permute-done.17.state_ref = bf16[64,4096]{1,0:T(8,128)(2,1)S(1)} collective-permute-done((bf16[64,4096]{1,0:T(8,128)(2,1)S(1)}, bf16[64,4096]{1,0:T(8,128)(2,1)S(1)}, u32[]{:S(2)}, u32[]{:S(2)}) %collective-permute-start.17) | collective-permute-done | bytes 524320 | tf_op jit(solution)/shard_map/ppermute | solution.py:45
  202.2 3.4 collective-permute-start.29
  205.6 8.3 %collective-permute-done.28.refs_2_ = bf16[64,4224]{1,0:T(8,128)(2,1)S(1)} collective-permute-done((bf16[64,4224]{1,0:T(8,128)(2,1)S(1)}, bf16[64,4224]{1,0:T(8,128)(2,1)S(1)}, u32[]{:S(2)}, u32[]{:S(2)}) %collective-permute-start.28) | collective-permute-done | bytes 540704 | tf_op jit(solution)/shard_map/ppermute | solution.py:40
  215.3 10.0 %collective-permute-done.27.state_ref = bf16[64,4096]{1,0:T(8,128)(2,1)S(1)} collective-permute-done((bf16[64,4096]{1,0:T(8,128)(2,1)S(1)}, bf16[64,4096]{1,0:T(8,128)(2,1)S(1)}, u32[]{:S(2)}, u32[]{:S(2)}) %collective-permute-start.27) | collective-permute-done | bytes 524320 | tf_op jit(solution)/shard_map/ppermute | solution.py:45
  225.6 3.5 collective-permute-start.35
  231.8 2.8 collective-permute-start.34
  234.5 3.9 %collective-permute-done.35.refs_3_ = bf16[64,4224]{1,0:T(8,128)(2,1)S(1)} collective-permute-done((bf16[64,4224]{1,0:T(8,128)(2,1)S(1)}, bf16[64,4224]{1,0:T(8,128)(2,1)S(1)}, u32[]{:S(2)}, u32[]{:S(2)}) %collective-permute-start.35) | collective-permute-done | bytes 540704 | tf_op jit(solution)/shard_map/ppermute | solution.py:40
  241.1 3.1 collective-permute-done.33.refs_7_
  244.2 9.6 %up.6.hidden_ref = bf16[512,1536]{1,0:T(8,128)(2,1)S(1)} custom-call(f32[2,128]{1,0:T(2,128)S(1)} %and_convert_fusion.refs_0_, bf16[64,4224]{1,0:T(8,128)(2,1)S(1)} %norm.7.refs_1_, bf16[64,4224]{1,0:T(8,128)(2,1)S(1)} %collective-permute-done.28.refs_2_, bf16[64,4224]{1,0:T(8,128)(2,1)S(1)} %collective-permute-done.29.refs_3_, ...), custom_call_target="tpu_custom_call" | custom-call | flops 6442450944 | bytes 18350080 | tf_op jit(solution)/shard_map/up/pallas_call | solution.py:110
  253.8 9.4 %down.6 = (bf16[64,4096]{1,0:T(8,128)(2,1)S(1)}, bf16[64,4096]{1,0:T(8,128)(2,1)S(1)}, bf16[64,4096]{1,0:T(8,128)(2,1)S(1)}, bf16[64,4096]{1,0:T(8,128)(2,1)S(1)...) custom-call(bf16[512,1536]{1,0:T(8,128)(2,1)S(1)} %up.6.hidden_ref, ...), custom_call_target="tpu_custom_call" | custom-call | flops 6442450944 | bytes 18350080 | tf_op jit(solution)/shard_map/down/pallas_call | solution.py:140
  265.6 3.1 collective-permute-start.46
  268.9 10.6 %collective-permute-done.37 = bf16[64,4096]{1,0:T(8,128)(2,1)S(1)} collective-permute-done((bf16[64,4096]{1,0:T(8,128)(2,1)S(1)}, bf16[64,4096]{1,0:T(8,128)(2,1)S(1)}, u32[]{:S(2)}, u32[]{:S(2)}) %collective-permute-start.37) | collective-permute-done | bytes 524320 | tf_op jit(solution)/shard_map/ppermute | solution.py:40
  279.6 2.9 collective-permute-start.38
  282.5 9.8 %collective-permute-done.44.refs_5_ = bf16[128,4224]{1,0:T(8,128)(2,1)S(1)} collective-permute-done((bf16[128,4224]{1,0:T(8,128)(2,1)S(1)}, bf16[128,4224]{1,0:T(8,128)(2,1)S(1)}, u32[]{:S(2)}, u32[]{:S(2)}) %collective-permute-start.44) | collective-permute-done | bytes 1081376 | tf_op jit(solution)/shard_map/ppermute | solution.py:40
  292.3 9.6 %up.7.hidden_ref = bf16[512,1536]{1,0:T(8,128)(2,1)S(1)} custom-call(f32[2,128]{1,0:T(2,128)S(1)} %and_convert_fusion.refs_0_, bf16[64,4224]{1,0:T(8,128)(2,1)S(1)} %norm.6.refs_1_, bf16[64,4224]{1,0:T(8,128)(2,1)S(1)} %collective-permute-done.34.refs_2_, bf16[64,4224]{1,0:T(8,128)(2,1)S(1)} %collective-permute-done.35.refs_3_, ...), custom_call_target="tpu_custom_call" | custom-call | flops 6442450944 | bytes 18350080 | tf_op jit(solution)/shard_map/up/pallas_call | solution.py:110
  302.3 9.4 %down.7 = (bf16[64,4096]{1,0:T(8,128)(2,1)S(1)}, bf16[64,4096]{1,0:T(8,128)(2,1)S(1)}, bf16[64,4096]{1,0:T(8,128)(2,1)S(1)}, bf16[64,4096]{1,0:T(8,128)(2,1)S(1)...) custom-call(bf16[512,1536]{1,0:T(8,128)(2,1)S(1)} %up.7.hidden_ref, ...), custom_call_target="tpu_custom_call" | custom-call | flops 6442450944 | bytes 18350080 | tf_op jit(solution)/shard_map/down/pallas_call | solution.py:140
  311.8 14.7 %collective-permute-done.47 = bf16[64,4096]{1,0:T(8,128)(2,1)S(1)} collective-permute-done((bf16[64,4096]{1,0:T(8,128)(2,1)S(1)}, bf16[64,4096]{1,0:T(8,128)(2,1)S(1)}, u32[]{:S(2)}, u32[]{:S(2)}) %collective-permute-start.47) | collective-permute-done | bytes 524320 | tf_op jit(solution)/shard_map/ppermute | solution.py:40
  332.3 7.9 %collective-permute-done.48 = bf16[64,4096]{1,0:T(8,128)(2,1)S(1)} collective-permute-done((bf16[64,4096]{1,0:T(8,128)(2,1)S(1)}, bf16[64,4096]{1,0:T(8,128)(2,1)S(1)}, u32[]{:S(2)}, u32[]{:S(2)}) %collective-permute-start.48) | collective-permute-done | bytes 524320 | tf_op jit(solution)/shard_map/ppermute | solution.py:40
  340.5 7.0 %collective-permute-done.50 = bf16[128,4096]{1,0:T(8,128)(2,1)S(1)} collective-permute-done((bf16[128,4096]{1,0:T(8,128)(2,1)S(1)}, bf16[128,4096]{1,0:T(8,128)(2,1)S(1)}, u32[]{:S(2)}, u32[]{:S(2)}) %collective-permute-start.50) | collective-permute-done | bytes 1048608 | tf_op jit(solution)/shard_map/ppermute | solution.py:40
  349.9 3.2 collective-permute-done.41
  353.1 3.2 collective-permute-start.52
  358.7 5.1 %collective-permute-done.52 = bf16[64,4096]{1,0:T(8,128)(2,1)S(1)} collective-permute-done((bf16[64,4096]{1,0:T(8,128)(2,1)S(1)}, bf16[64,4096]{1,0:T(8,128)(2,1)S(1)}, u32[]{:S(2)}, u32[]{:S(2)}) %collective-permute-start.52) | collective-permute-done | bytes 524320 | tf_op jit(solution)/shard_map/ppermute | solution.py:40
  364.2 2.9 collective-permute-done.43
  367.1 7.5 %collective-permute-done.53 = bf16[64,4096]{1,0:T(8,128)(2,1)S(1)} collective-permute-done((bf16[64,4096]{1,0:T(8,128)(2,1)S(1)}, bf16[64,4096]{1,0:T(8,128)(2,1)S(1)}, u32[]{:S(2)}, u32[]{:S(2)}) %collective-permute-start.53) | collective-permute-done | bytes 524320 | tf_op jit(solution)/shard_map/ppermute | solution.py:45
  (122 shorter events, 47.4 us)
Async XLA Ops:
  0.0 64.5 %collective-permute-start.6 = (bf16[4096,768]{1,0:T(8,128)(2,1)}, bf16[4096,768]{1,0:T(8,128)(2,1)}, u32[]{:S(2)}, u32[]{:S(2)}) collective-permute-start(bf16[4096,768]{1,0:T(8,128)(2,1)} %bitcast.17), channel_id=1, source_target_pairs={{0,2},{2,0},{4,6},{6,4},{8,10},{10,8},{12,14},{14,12},{16,18},{18,... | collective-permute-start | bytes 18874376 | tf_op jit(solution)/shard_map/ppermute | solution.py:40
  0.0 78.7 %collective-permute-start.10 = (bf16[768,4096]{1,0:T(8,128)(2,1)}, bf16[768,4096]{1,0:T(8,128)(2,1)}, u32[]{:S(2)}, u32[]{:S(2)}) collective-permute-start(bf16[768,4096]{1,0:T(8,128)(2,1)} %bitcast.24), channel_id=1, source_target_pairs={{0,2},{2,0},{4,6},{6,4},{8,10},{10,8},{12,14},{14,12},{16,18},{18,... | collective-permute-start | bytes 18874376 | tf_op jit(solution)/shard_map/ppermute | solution.py:40
  5.2 14.6 %collective-permute-start.1 = (bf16[64,4224]{1,0:T(8,128)(2,1)S(1)}, bf16[64,4224]{1,0:T(8,128)(2,1)S(1)}, u32[]{:S(2)}, u32[]{:S(2)}) collective-permute-start(bf16[64,4224]{1,0:T(8,128)(2,1)S(1)} %norm.4.refs_1_), channel_id=1, source_target_pairs={{0,24},{2,26},{4,28},{6,30},{8,0},{10,2},{12,4},{14,6},{16,8},{18,... | collective-permute-start | bytes 1622024 | tf_op jit(solution)/shard_map/ppermute | solution.py:40
  8.1 15.6 %collective-permute-start = (bf16[64,4224]{1,0:T(8,128)(2,1)S(1)}, bf16[64,4224]{1,0:T(8,128)(2,1)S(1)}, u32[]{:S(2)}, u32[]{:S(2)}) collective-permute-start(bf16[64,4224]{1,0:T(8,128)(2,1)S(1)} %norm.4.refs_1_), channel_id=1, source_target_pairs={{0,8},{2,10},{4,12},{6,14},{8,16},{10,18},{12,20},{14,22},{16,24},... | collective-permute-start | bytes 1622024 | tf_op jit(solution)/shard_map/ppermute | solution.py:40
  8.1 16.4 %collective-permute-start.2 = (bf16[64,4224]{1,0:T(8,128)(2,1)S(1)}, bf16[64,4224]{1,0:T(8,128)(2,1)S(1)}, u32[]{:S(2)}, u32[]{:S(2)}) collective-permute-start(bf16[64,4224]{1,0:T(8,128)(2,1)S(1)} %norm.4.refs_1_), channel_id=1, source_target_pairs={{0,4},{2,6},{4,0},{6,2},{8,12},{10,14},{12,8},{14,10},{16,20},{18,... | collective-permute-start | bytes 1622024 | tf_op jit(solution)/shard_map/ppermute | solution.py:40
  19.8 16.0 %collective-permute-start.4 = (bf16[64,4224]{1,0:T(8,128)(2,1)S(1)}, bf16[64,4224]{1,0:T(8,128)(2,1)}, u32[]{:S(2)}, u32[]{:S(2)}) collective-permute-start(bf16[64,4224]{1,0:T(8,128)(2,1)S(1)} %collective-permute-done.1.refs_3_), channel_id=1, source_target_pairs={{0,4},{2,6},{4,0},{6,2},{8,12},{10,14},{12,8},{14,10},{16,20},{18,... | collective-permute-start | bytes 1622024 | tf_op jit(solution)/shard_map/ppermute | solution.py:40
  25.6 26.1 %collective-permute-start.3 = (bf16[128,4224]{1,0:T(8,128)(2,1)}, bf16[128,4224]{1,0:T(8,128)(2,1)}, u32[]{:S(2)}, u32[]{:S(2)}) collective-permute-start(bf16[128,4224]{1,0:T(8,128)(2,1)} %pad_maximum_fusion), channel_id=1, source_target_pairs={{0,8},{2,10},{4,12},{6,14},{8,16},{10,18},{12,20},{14,22},{16,24},... | collective-permute-start | bytes 3244040 | tf_op jit(solution)/shard_map/ppermute | solution.py:40
  35.8 16.3 %collective-permute-start.5 = (bf16[64,4224]{1,0:T(8,128)(2,1)}, bf16[64,4224]{1,0:T(8,128)(2,1)}, u32[]{:S(2)}, u32[]{:S(2)}) collective-permute-start(bf16[64,4224]{1,0:T(8,128)(2,1)} %collective-permute-done.4.refs_6_), channel_id=1, source_target_pairs={{0,24},{2,26},{4,28},{6,30},{8,0},{10,2},{12,4},{14,6},{16,8},{18,... | collective-permute-start | bytes 1622024 | tf_op jit(solution)/shard_map/ppermute | solution.py:40
  39.1 22.0 %collective-permute-start.8 = (bf16[64,4224]{1,0:T(8,128)(2,1)S(1)}, bf16[64,4224]{1,0:T(8,128)(2,1)}, u32[]{:S(2)}, u32[]{:S(2)}) collective-permute-start(bf16[64,4224]{1,0:T(8,128)(2,1)S(1)} %norm.5.refs_1_), channel_id=1, source_target_pairs={{0,24},{2,26},{4,28},{6,30},{8,0},{10,2},{12,4},{14,6},{16,8},{18,... | collective-permute-start | bytes 1622024 | tf_op jit(solution)/shard_map/ppermute | solution.py:40
  51.7 27.0 %collective-permute-start.7 = (bf16[64,4224]{1,0:T(8,128)(2,1)S(1)}, bf16[64,4224]{1,0:T(8,128)(2,1)S(1)}, u32[]{:S(2)}, u32[]{:S(2)}) collective-permute-start(bf16[64,4224]{1,0:T(8,128)(2,1)S(1)} %norm.5.refs_1_), channel_id=1, source_target_pairs={{0,8},{2,10},{4,12},{6,14},{8,16},{10,18},{12,20},{14,22},{16,24},... | collective-permute-start | bytes 1622024 | tf_op jit(solution)/shard_map/ppermute | solution.py:40
  52.1 26.6 %collective-permute-start.9 = (bf16[64,4224]{1,0:T(8,128)(2,1)S(1)}, bf16[64,4224]{1,0:T(8,128)(2,1)S(1)}, u32[]{:S(2)}, u32[]{:S(2)}) collective-permute-start(bf16[64,4224]{1,0:T(8,128)(2,1)S(1)} %norm.5.refs_1_), channel_id=1, source_target_pairs={{0,4},{2,6},{4,0},{6,2},{8,12},{10,14},{12,8},{14,10},{16,20},{18,... | collective-permute-start | bytes 1622024 | tf_op jit(solution)/shard_map/ppermute | solution.py:40
  61.1 29.8 %collective-permute-start.19 = (bf16[64,4224]{1,0:T(8,128)(2,1)}, bf16[64,4224]{1,0:T(8,128)(2,1)S(1)}, u32[]{:S(2)}, u32[]{:S(2)}) collective-permute-start(bf16[64,4224]{1,0:T(8,128)(2,1)} %collective-permute-done.8.refs_3_), channel_id=1, source_target_pairs={{0,4},{2,6},{4,0},{6,2},{8,12},{10,14},{12,8},{14,10},{16,20},{18,... | collective-permute-start | bytes 1622024 | tf_op jit(solution)/shard_map/ppermute | solution.py:40
  88.4 16.7 %collective-permute-start.11 = (bf16[64,4096]{1,0:T(8,128)(2,1)S(1)}, bf16[64,4096]{1,0:T(8,128)(2,1)S(1)}, u32[]{:S(2)}, u32[]{:S(2)}) collective-permute-start(bf16[64,4096]{1,0:T(8,128)(2,1)S(1)} %get-tuple-element.46), channel_id=1, source_target_pairs={{0,8},{2,10},{4,12},{6,14},{8,16},{10,18},{12,20},{14,22},{16,24},... | collective-permute-start | bytes 1572872 | tf_op jit(solution)/shard_map/ppermute | solution.py:40
  88.7 35.9 %collective-permute-start.18 = (bf16[128,4224]{1,0:T(8,128)(2,1)S(1)}, bf16[128,4224]{1,0:T(8,128)(2,1)S(1)}, u32[]{:S(2)}, u32[]{:S(2)}) collective-permute-start(bf16[128,4224]{1,0:T(8,128)(2,1)S(1)} %pad_maximum_fusion.1), channel_id=1, source_target_pairs={{0,8},{2,10},{4,12},{6,14},{8,16},{10,18},{12,20},{14,22},{16,24},... | collective-permute-start | bytes 3244040 | tf_op jit(solution)/shard_map/ppermute | solution.py:40
  90.9 33.7 %collective-permute-start.20 = (bf16[64,4224]{1,0:T(8,128)(2,1)S(1)}, bf16[64,4224]{1,0:T(8,128)(2,1)S(1)}, u32[]{:S(2)}, u32[]{:S(2)}) collective-permute-start(bf16[64,4224]{1,0:T(8,128)(2,1)S(1)} %collective-permute-done.19.refs_6_), channel_id=1, source_target_pairs={{0,24},{2,26},{4,28},{6,30},{8,0},{10,2},{12,4},{14,6},{16,8},{18,... | collective-permute-start | bytes 1622024 | tf_op jit(solution)/shard_map/ppermute | solution.py:40
  92.5 42.0 %collective-permute-start.14 = (bf16[128,4096]{1,0:T(8,128)(2,1)S(1)}, bf16[128,4096]{1,0:T(8,128)(2,1)S(1)}, u32[]{:S(2)}, u32[]{:S(2)}) collective-permute-start(bf16[128,4096]{1,0:T(8,128)(2,1)S(1)} %get-tuple-element.48), channel_id=1, source_target_pairs={{0,24},{2,26},{4,28},{6,30},{8,0},{10,2},{12,4},{14,6},{16,8},{18,... | collective-permute-start | bytes 3145736 | tf_op jit(solution)/shard_map/ppermute | solution.py:40
  105.3 29.1 %collective-permute-start.12 = (bf16[64,4096]{1,0:T(8,128)(2,1)S(1)}, bf16[64,4096]{1,0:T(8,128)(2,1)S(1)}, u32[]{:S(2)}, u32[]{:S(2)}) collective-permute-start(bf16[64,4096]{1,0:T(8,128)(2,1)S(1)} %add_convert_fusion.17), channel_id=1, source_target_pairs={{0,4},{2,6},{4,0},{6,2},{8,12},{10,14},{12,8},{14,10},{16,20},{18,... | collective-permute-start | bytes 1572872 | tf_op jit(solution)/shard_map/ppermute | solution.py:40
  144.4 16.1 %collective-permute-start.21 = (bf16[64,4096]{1,0:T(8,128)(2,1)S(1)}, bf16[64,4096]{1,0:T(8,128)(2,1)S(1)}, u32[]{:S(2)}, u32[]{:S(2)}) collective-permute-start(bf16[64,4096]{1,0:T(8,128)(2,1)S(1)} %get-tuple-element.55), channel_id=1, source_target_pairs={{0,8},{2,10},{4,12},{6,14},{8,16},{10,18},{12,20},{14,22},{16,24},... | collective-permute-start | bytes 1572872 | tf_op jit(solution)/shard_map/ppermute | solution.py:40
  144.4 26.8 %collective-permute-start.24 = (bf16[128,4096]{1,0:T(8,128)(2,1)S(1)}, bf16[128,4096]{1,0:T(8,128)(2,1)S(1)}, u32[]{:S(2)}, u32[]{:S(2)}) collective-permute-start(bf16[128,4096]{1,0:T(8,128)(2,1)S(1)} %get-tuple-element.57), channel_id=1, source_target_pairs={{0,24},{2,26},{4,28},{6,30},{8,0},{10,2},{12,4},{14,6},{16,8},{18,... | collective-permute-start | bytes 3145736 | tf_op jit(solution)/shard_map/ppermute | solution.py:40
  147.7 28.6 %collective-permute-start.13 = (bf16[64,4096]{1,0:T(8,128)(2,1)S(1)}, bf16[64,4096]{1,0:T(8,128)(2,1)S(1)}, u32[]{:S(2)}, u32[]{:S(2)}) collective-permute-start(bf16[64,4096]{1,0:T(8,128)(2,1)S(1)} %add_convert_fusion.16), channel_id=1, source_target_pairs={{0,8},{2,10},{4,12},{6,14},{8,16},{10,18},{12,20},{14,22},{16,24},... | collective-permute-start | bytes 1572872 | tf_op jit(solution)/shard_map/ppermute | solution.py:40
  147.7 34.8 %collective-permute-start.15 = (bf16[64,4096]{1,0:T(8,128)(2,1)S(1)}, bf16[64,4096]{1,0:T(8,128)(2,1)S(1)}, u32[]{:S(2)}, u32[]{:S(2)}) collective-permute-start(bf16[64,4096]{1,0:T(8,128)(2,1)S(1)} %get-tuple-element.86), channel_id=1, source_target_pairs={{0,24},{2,26},{4,28},{6,30},{8,0},{10,2},{12,4},{14,6},{16,8},{18,... | collective-permute-start | bytes 1572872 | tf_op jit(solution)/shard_map/ppermute | solution.py:40
  150.9 31.6 %collective-permute-start.16 = (bf16[64,4096]{1,0:T(8,128)(2,1)S(1)}, bf16[64,4096]{1,0:T(8,128)(2,1)S(1)}, u32[]{:S(2)}, u32[]{:S(2)}) collective-permute-start(bf16[64,4096]{1,0:T(8,128)(2,1)S(1)} %get-tuple-element.85), channel_id=1, source_target_pairs={{0,4},{2,6},{4,0},{6,2},{8,12},{10,14},{12,8},{14,10},{16,20},{18,... | collective-permute-start | bytes 1572872 | tf_op jit(solution)/shard_map/ppermute | solution.py:40
  160.6 14.7 %collective-permute-start.22 = (bf16[64,4096]{1,0:T(8,128)(2,1)S(1)}, bf16[64,4096]{1,0:T(8,128)(2,1)S(1)}, u32[]{:S(2)}, u32[]{:S(2)}) collective-permute-start(bf16[64,4096]{1,0:T(8,128)(2,1)S(1)} %add_convert_fusion.13), channel_id=1, source_target_pairs={{0,4},{2,6},{4,0},{6,2},{8,12},{10,14},{12,8},{14,10},{16,20},{18,... | collective-permute-start | bytes 1572872 | tf_op jit(solution)/shard_map/ppermute | solution.py:40
  171.5 17.3 %collective-permute-start.25 = (bf16[64,4096]{1,0:T(8,128)(2,1)S(1)}, bf16[64,4096]{1,0:T(8,128)(2,1)S(1)}, u32[]{:S(2)}, u32[]{:S(2)}) collective-permute-start(bf16[64,4096]{1,0:T(8,128)(2,1)S(1)} %get-tuple-element.83), channel_id=1, source_target_pairs={{0,24},{2,26},{4,28},{6,30},{8,0},{10,2},{12,4},{14,6},{16,8},{18,... | collective-permute-start | bytes 1572872 | tf_op jit(solution)/shard_map/ppermute | solution.py:40
  175.3 13.5 %collective-permute-start.26 = (bf16[64,4096]{1,0:T(8,128)(2,1)S(1)}, bf16[64,4096]{1,0:T(8,128)(2,1)S(1)}, u32[]{:S(2)}, u32[]{:S(2)}) collective-permute-start(bf16[64,4096]{1,0:T(8,128)(2,1)S(1)} %get-tuple-element.84), channel_id=1, source_target_pairs={{0,4},{2,6},{4,0},{6,2},{8,12},{10,14},{12,8},{14,10},{16,20},{18,... | collective-permute-start | bytes 1572872 | tf_op jit(solution)/shard_map/ppermute | solution.py:40
  176.3 12.5 %collective-permute-start.23 = (bf16[64,4096]{1,0:T(8,128)(2,1)S(1)}, bf16[64,4096]{1,0:T(8,128)(2,1)S(1)}, u32[]{:S(2)}, u32[]{:S(2)}) collective-permute-start(bf16[64,4096]{1,0:T(8,128)(2,1)S(1)} %add_convert_fusion.12), channel_id=1, source_target_pairs={{0,8},{2,10},{4,12},{6,14},{8,16},{10,18},{12,20},{14,22},{16,24},... | collective-permute-start | bytes 1572872 | tf_op jit(solution)/shard_map/ppermute | solution.py:40
  200.4 13.5 %collective-permute-start.28 = (bf16[64,4224]{1,0:T(8,128)(2,1)S(1)}, bf16[64,4224]{1,0:T(8,128)(2,1)S(1)}, u32[]{:S(2)}, u32[]{:S(2)}) collective-permute-start(bf16[64,4224]{1,0:T(8,128)(2,1)S(1)} %norm.7.refs_1_), channel_id=1, source_target_pairs={{0,8},{2,10},{4,12},{6,14},{8,16},{10,18},{12,20},{14,22},{16,24},... | collective-permute-start | bytes 1622024 | tf_op jit(solution)/shard_map/ppermute | solution.py:40
  200.9 13.0 %collective-permute-start.30 = (bf16[64,4224]{1,0:T(8,128)(2,1)S(1)}, bf16[64,4224]{1,0:T(8,128)(2,1)S(1)}, u32[]{:S(2)}, u32[]{:S(2)}) collective-permute-start(bf16[64,4224]{1,0:T(8,128)(2,1)S(1)} %norm.7.refs_1_), channel_id=1, source_target_pairs={{0,4},{2,6},{4,0},{6,2},{8,12},{10,14},{12,8},{14,10},{16,20},{18,... | collective-permute-start | bytes 1622024 | tf_op jit(solution)/shard_map/ppermute | solution.py:40
  202.2 11.9 %collective-permute-start.29 = (bf16[64,4224]{1,0:T(8,128)(2,1)S(1)}, bf16[64,4224]{1,0:T(8,128)(2,1)S(1)}, u32[]{:S(2)}, u32[]{:S(2)}) collective-permute-start(bf16[64,4224]{1,0:T(8,128)(2,1)S(1)} %norm.7.refs_1_), channel_id=1, source_target_pairs={{0,24},{2,26},{4,28},{6,30},{8,0},{10,2},{12,4},{14,6},{16,8},{18,... | collective-permute-start | bytes 1622024 | tf_op jit(solution)/shard_map/ppermute | solution.py:40
  214.0 27.1 %collective-permute-start.31 = (bf16[128,4224]{1,0:T(8,128)(2,1)S(1)}, bf16[128,4224]{1,0:T(8,128)(2,1)S(1)}, u32[]{:S(2)}, u32[]{:S(2)}) collective-permute-start(bf16[128,4224]{1,0:T(8,128)(2,1)S(1)} %pad_maximum_fusion.2), channel_id=1, source_target_pairs={{0,8},{2,10},{4,12},{6,14},{8,16},{10,18},{12,20},{14,22},{16,24},... | collective-permute-start | bytes 3244040 | tf_op jit(solution)/shard_map/ppermute | solution.py:40
  214.1 15.0 %collective-permute-start.32 = (bf16[64,4224]{1,0:T(8,128)(2,1)S(1)}, bf16[64,4224]{1,0:T(8,128)(2,1)S(1)}, u32[]{:S(2)}, u32[]{:S(2)}) collective-permute-start(bf16[64,4224]{1,0:T(8,128)(2,1)S(1)} %collective-permute-done.29.refs_3_), channel_id=1, source_target_pairs={{0,4},{2,6},{4,0},{6,2},{8,12},{10,14},{12,8},{14,10},{16,20},{18,... | collective-permute-start | bytes 1622024 | tf_op jit(solution)/shard_map/ppermute | solution.py:40
  225.6 12.8 %collective-permute-start.35 = (bf16[64,4224]{1,0:T(8,128)(2,1)S(1)}, bf16[64,4224]{1,0:T(8,128)(2,1)S(1)}, u32[]{:S(2)}, u32[]{:S(2)}) collective-permute-start(bf16[64,4224]{1,0:T(8,128)(2,1)S(1)} %norm.6.refs_1_), channel_id=1, source_target_pairs={{0,24},{2,26},{4,28},{6,30},{8,0},{10,2},{12,4},{14,6},{16,8},{18,... | collective-permute-start | bytes 1622024 | tf_op jit(solution)/shard_map/ppermute | solution.py:40
  229.1 15.1 %collective-permute-start.33 = (bf16[64,4224]{1,0:T(8,128)(2,1)S(1)}, bf16[64,4224]{1,0:T(8,128)(2,1)S(1)}, u32[]{:S(2)}, u32[]{:S(2)}) collective-permute-start(bf16[64,4224]{1,0:T(8,128)(2,1)S(1)} %collective-permute-done.32.refs_6_), channel_id=1, source_target_pairs={{0,24},{2,26},{4,28},{6,30},{8,0},{10,2},{12,4},{14,6},{16,8},{18,... | collective-permute-start | bytes 1622024 | tf_op jit(solution)/shard_map/ppermute | solution.py:40
  231.8 22.0 %collective-permute-start.34 = (bf16[64,4224]{1,0:T(8,128)(2,1)S(1)}, bf16[64,4224]{1,0:T(8,128)(2,1)S(1)}, u32[]{:S(2)}, u32[]{:S(2)}) collective-permute-start(bf16[64,4224]{1,0:T(8,128)(2,1)S(1)} %norm.6.refs_1_), channel_id=1, source_target_pairs={{0,8},{2,10},{4,12},{6,14},{8,16},{10,18},{12,20},{14,22},{16,24},... | collective-permute-start | bytes 1622024 | tf_op jit(solution)/shard_map/ppermute | solution.py:40
  234.5 19.3 %collective-permute-start.36 = (bf16[64,4224]{1,0:T(8,128)(2,1)S(1)}, bf16[64,4224]{1,0:T(8,128)(2,1)S(1)}, u32[]{:S(2)}, u32[]{:S(2)}) collective-permute-start(bf16[64,4224]{1,0:T(8,128)(2,1)S(1)} %norm.6.refs_1_), channel_id=1, source_target_pairs={{0,4},{2,6},{4,0},{6,2},{8,12},{10,14},{12,8},{14,10},{16,20},{18,... | collective-permute-start | bytes 1622024 | tf_op jit(solution)/shard_map/ppermute | solution.py:40
  238.4 27.2 %collective-permute-start.45 = (bf16[64,4224]{1,0:T(8,128)(2,1)S(1)}, bf16[64,4224]{1,0:T(8,128)(2,1)S(1)}, u32[]{:S(2)}, u32[]{:S(2)}) collective-permute-start(bf16[64,4224]{1,0:T(8,128)(2,1)S(1)} %collective-permute-done.35.refs_3_), channel_id=1, source_target_pairs={{0,4},{2,6},{4,0},{6,2},{8,12},{10,14},{12,8},{14,10},{16,20},{18,... | collective-permute-start | bytes 1622024 | tf_op jit(solution)/shard_map/ppermute | solution.py:40
  263.3 16.2 %collective-permute-start.37 = (bf16[64,4096]{1,0:T(8,128)(2,1)S(1)}, bf16[64,4096]{1,0:T(8,128)(2,1)S(1)}, u32[]{:S(2)}, u32[]{:S(2)}) collective-permute-start(bf16[64,4096]{1,0:T(8,128)(2,1)S(1)} %get-tuple-element.64), channel_id=1, source_target_pairs={{0,8},{2,10},{4,12},{6,14},{8,16},{10,18},{12,20},{14,22},{16,24},... | collective-permute-start | bytes 1572872 | tf_op jit(solution)/shard_map/ppermute | solution.py:40
  265.4 26.9 %collective-permute-start.44 = (bf16[128,4224]{1,0:T(8,128)(2,1)S(1)}, bf16[128,4224]{1,0:T(8,128)(2,1)S(1)}, u32[]{:S(2)}, u32[]{:S(2)}) collective-permute-start(bf16[128,4224]{1,0:T(8,128)(2,1)S(1)} %pad_maximum_fusion.3), channel_id=1, source_target_pairs={{0,8},{2,10},{4,12},{6,14},{8,16},{10,18},{12,20},{14,22},{16,24},... | collective-permute-start | bytes 3244040 | tf_op jit(solution)/shard_map/ppermute | solution.py:40
  265.6 26.7 %collective-permute-start.46 = (bf16[64,4224]{1,0:T(8,128)(2,1)S(1)}, bf16[64,4224]{1,0:T(8,128)(2,1)S(1)}, u32[]{:S(2)}, u32[]{:S(2)}) collective-permute-start(bf16[64,4224]{1,0:T(8,128)(2,1)S(1)} %collective-permute-done.45.refs_6_), channel_id=1, source_target_pairs={{0,24},{2,26},{4,28},{6,30},{8,0},{10,2},{12,4},{14,6},{16,8},{18,... | collective-permute-start | bytes 1622024 | tf_op jit(solution)/shard_map/ppermute | solution.py:40
  268.8 33.1 %collective-permute-start.40 = (bf16[128,4096]{1,0:T(8,128)(2,1)S(1)}, bf16[128,4096]{1,0:T(8,128)(2,1)S(1)}, u32[]{:S(2)}, u32[]{:S(2)}) collective-permute-start(bf16[128,4096]{1,0:T(8,128)(2,1)S(1)} %get-tuple-element.66), channel_id=1, source_target_pairs={{0,24},{2,26},{4,28},{6,30},{8,0},{10,2},{12,4},{14,6},{16,8},{18,... | collective-permute-start | bytes 3145736 | tf_op jit(solution)/shard_map/ppermute | solution.py:40
  279.6 22.6 %collective-permute-start.38 = (bf16[64,4096]{1,0:T(8,128)(2,1)S(1)}, bf16[64,4096]{1,0:T(8,128)(2,1)S(1)}, u32[]{:S(2)}, u32[]{:S(2)}) collective-permute-start(bf16[64,4096]{1,0:T(8,128)(2,1)S(1)} %add_convert_fusion.9), channel_id=1, source_target_pairs={{0,4},{2,6},{4,0},{6,2},{8,12},{10,14},{12,8},{14,10},{16,20},{18,... | collective-permute-start | bytes 1572872 | tf_op jit(solution)/shard_map/ppermute | solution.py:40
  311.8 14.8 %collective-permute-start.47 = (bf16[64,4096]{1,0:T(8,128)(2,1)S(1)}, bf16[64,4096]{1,0:T(8,128)(2,1)S(1)}, u32[]{:S(2)}, u32[]{:S(2)}) collective-permute-start(bf16[64,4096]{1,0:T(8,128)(2,1)S(1)} %get-tuple-element.73), channel_id=1, source_target_pairs={{0,8},{2,10},{4,12},{6,14},{8,16},{10,18},{12,20},{14,22},{16,24},... | collective-permute-start | bytes 1572872 | tf_op jit(solution)/shard_map/ppermute | solution.py:40
  326.7 13.6 %collective-permute-start.48 = (bf16[64,4096]{1,0:T(8,128)(2,1)S(1)}, bf16[64,4096]{1,0:T(8,128)(2,1)S(1)}, u32[]{:S(2)}, u32[]{:S(2)}) collective-permute-start(bf16[64,4096]{1,0:T(8,128)(2,1)S(1)} %add_convert_fusion.4), channel_id=1, source_target_pairs={{0,4},{2,6},{4,0},{6,2},{8,12},{10,14},{12,8},{14,10},{16,20},{18,... | collective-permute-start | bytes 1572872 | tf_op jit(solution)/shard_map/ppermute | solution.py:40
  328.8 18.7 %collective-permute-start.50 = (bf16[128,4096]{1,0:T(8,128)(2,1)S(1)}, bf16[128,4096]{1,0:T(8,128)(2,1)S(1)}, u32[]{:S(2)}, u32[]{:S(2)}) collective-permute-start(bf16[128,4096]{1,0:T(8,128)(2,1)S(1)} %get-tuple-element.75), channel_id=1, source_target_pairs={{0,24},{2,26},{4,28},{6,30},{8,0},{10,2},{12,4},{14,6},{16,8},{18,... | collective-permute-start | bytes 3145736 | tf_op jit(solution)/shard_map/ppermute | solution.py:40
  329.4 23.7 %collective-permute-start.41 = (bf16[64,4096]{1,0:T(8,128)(2,1)S(1)}, bf16[64,4096]{1,0:T(8,128)(2,1)S(1)}, u32[]{:S(2)}, u32[]{:S(2)}) collective-permute-start(bf16[64,4096]{1,0:T(8,128)(2,1)S(1)} %get-tuple-element.80), channel_id=1, source_target_pairs={{0,24},{2,26},{4,28},{6,30},{8,0},{10,2},{12,4},{14,6},{16,8},{18,... | collective-permute-start | bytes 1572872 | tf_op jit(solution)/shard_map/ppermute | solution.py:40
  329.4 26.8 %collective-permute-start.42 = (bf16[64,4096]{1,0:T(8,128)(2,1)S(1)}, bf16[64,4096]{1,0:T(8,128)(2,1)S(1)}, u32[]{:S(2)}, u32[]{:S(2)}) collective-permute-start(bf16[64,4096]{1,0:T(8,128)(2,1)S(1)} %get-tuple-element.79), channel_id=1, source_target_pairs={{0,4},{2,6},{4,0},{6,2},{8,12},{10,14},{12,8},{14,10},{16,20},{18,... | collective-permute-start | bytes 1572872 | tf_op jit(solution)/shard_map/ppermute | solution.py:40
  330.3 26.0 %collective-permute-start.39 = (bf16[64,4096]{1,0:T(8,128)(2,1)S(1)}, bf16[64,4096]{1,0:T(8,128)(2,1)S(1)}, u32[]{:S(2)}, u32[]{:S(2)}) collective-permute-start(bf16[64,4096]{1,0:T(8,128)(2,1)S(1)} %add_convert_fusion.8), channel_id=1, source_target_pairs={{0,8},{2,10},{4,12},{6,14},{8,16},{10,18},{12,20},{14,22},{16,24},... | collective-permute-start | bytes 1572872 | tf_op jit(solution)/shard_map/ppermute | solution.py:40
  340.4 16.3 %collective-permute-start.49 = (bf16[64,4096]{1,0:T(8,128)(2,1)S(1)}, bf16[64,4096]{1,0:T(8,128)(2,1)S(1)}, u32[]{:S(2)}, u32[]{:S(2)}) collective-permute-start(bf16[64,4096]{1,0:T(8,128)(2,1)S(1)} %add_convert_fusion.3), channel_id=1, source_target_pairs={{0,8},{2,10},{4,12},{6,14},{8,16},{10,18},{12,20},{14,22},{16,24},... | collective-permute-start | bytes 1572872 | tf_op jit(solution)/shard_map/ppermute | solution.py:40
  (16 other events, 230.4 us)

commit v2 on v1

--- a/solution.py
+++ b/solution.py
@@ -36,8 +36,9 @@
 MOVES = moves()
 
 
-def send(value, way):
-    return lax.ppermute(value, "expert", MOVES[way])
+def send(value, way, k=None, what=""):
+    with jax.named_scope(f"{what}_{k.c}_{k.visit}" if k else way):
+        return lax.ppermute(value, "expert", MOVES[way])
 
 
 def next_section(value):
@@ -152,8 +153,41 @@
     )(hidden, own, sib)
 
 
-def plus(a, b):
-    return (a.astype(jnp.float32) + b.astype(jnp.float32)).astype(jnp.bfloat16)
+def plus_kernel(at, a_ref, b_ref, out_ref):
+    other = b_ref[at : at + a_ref.shape[0], :].astype(jnp.float32)
+    out_ref[...] = (a_ref[...].astype(jnp.float32) + other).astype(out_ref.dtype)
+
+
+def plus(a, b, at=0):
+    return pl.pallas_call(
+        functools.partial(plus_kernel, at),
+        in_specs=[WHOLE] * 2,
+        out_specs=WHOLE,
+        out_shape=jax.ShapeDtypeStruct(a.shape, a.dtype),
+        compiler_params=params(),
+        cost_estimate=pl.CostEstimate(flops=a.size, bytes_accessed=6 * a.size, transcendentals=0),
+        name="plus",
+    )(a, b)
+
+
+def finish_kernel(span, state_ref, *refs):
+    total = state_ref[span, :].astype(jnp.float32)
+    for ref in refs[:-1]:
+        total = total + ref[...].astype(jnp.float32)
+    refs[-1][...] = total.astype(refs[-1].dtype)
+
+
+def finish(state, span, *parts):
+    size = parts[0].size
+    return pl.pallas_call(
+        functools.partial(finish_kernel, span),
+        in_specs=[WHOLE] * (1 + len(parts)),
+        out_specs=WHOLE,
+        out_shape=jax.ShapeDtypeStruct(parts[0].shape, parts[0].dtype),
+        compiler_params=params(),
+        cost_estimate=pl.CostEstimate(flops=4 * size, bytes_accessed=12 * size, transcendentals=0),
+        name="finish",
+    )(state, *parts)
 
 
 def chunk_rows(sizes):
@@ -177,7 +211,6 @@
     served = jnp.stack([me, me + 1 - 2 * (me % NC)])
     masks = ((lane[None, :] % experts == served[:, None]) & (lane[None, :] < 2 * experts)).astype(jnp.float32)
 
-    states = [activations[0, span] for span in spans]
     rows = [norm_call(norm_kernel, 0, span, activations[0], norm_gain, lanes) for span in spans]
     up_sib = send(up_own, "sibling")
     down_sib = send(down_own, "sibling")
@@ -185,20 +218,22 @@
     class Chunk:
         pass
 
-    def gather_1(k):
-        k.left = send(k.rows, "right")
-        k.right = send(k.rows, "left")
-        k.across = send(k.rows, "across")
+    def gather_1(k, held_left=()):
+        k.right = send(k.rows, "left", k, "right")
+        k.across = send(k.rows, "across", k, "across")
+        k.left = send(after(k.rows, *held_left), "right", k, "left")
 
     def gather_2(k):
-        k.far_and_left = send(jnp.concatenate([k.left, k.across]), "right")
-        k.across_right = send(k.right, "across")
+        right = after(k.right, *swapped) if k.visit + k.c == 0 else k.right
+        k.across_right = send(right, "across", k, "across_right")
+        k.pair = jnp.concatenate([k.left, k.across])
+        k.far = send(k.pair, "right", k, "far_and_left")
 
     def gather_3(k):
-        k.across_far = send(k.across_right, "left")
+        k.across_far = send(k.across_right, "left", k, "across_far")
 
     def up(k, *held):
-        pieces = [k.rows, k.left, k.right, k.across, k.far_and_left, k.across_right, k.across_far]
+        pieces = [k.rows, k.left, k.right, k.across, k.far, k.across_right, k.across_far]
         k.hidden = up_call(after(masks, *held), pieces, up_own, up_sib)
 
     def down(k, *held):
@@ -206,23 +241,21 @@
         parts = down_call(after(k.hidden, *held), down_own, down_sib, sizes)
         k.p_own, k.p_left, k.p_right, k.p_across, k.p_far_and_left, k.p_across_right, k.p_across_far = parts
 
-    def return_1(k):
-        back = send(k.p_across_far, "right")
-        both = send(k.p_far_and_left, "left")
+    def return_1(k, held_back=(), held_both=()):
+        back = send(after(k.p_across_far, *held_back), "right", k, "back_1_far")
+        both = send(after(k.p_far_and_left, *held_both), "left", k, "back_1_both")
         k.s_across_right = plus(k.p_across_right, back)
-        k.s_left = plus(k.p_left, both[:chunk])
-        k.s_across = plus(k.p_across, both[chunk:])
+        k.s_left = plus(k.p_left, both)
+        k.s_across = plus(k.p_across, both, chunk)
 
     def return_2(k):
-        k.s_right = plus(k.p_right, send(k.s_across_right, "across"))
+        k.s_right = plus(k.p_right, send(k.s_across_right, "across", k, "back_2"))
 
     def return_3(k):
-        from_left = send(k.s_right, "right")
-        from_right = send(k.s_left, "left")
-        from_across = send(k.s_across, "across")
-        total = k.state.astype(jnp.float32) + k.p_own.astype(jnp.float32)
-        total = total + from_left.astype(jnp.float32) + from_right.astype(jnp.float32) + from_across.astype(jnp.float32)
-        k.mixed = total.astype(jnp.bfloat16)
+        k.from_left = send(k.s_right, "right", k, "back_3_right")
+        k.from_right = send(k.s_left, "left", k, "back_3_left")
+        k.from_across = send(k.s_across, "across", k, "back_3_across")
+        k.mixed = finish(k.state, k.span, k.p_own, k.from_left, k.from_right, k.from_across)
 
     def onward(k):
         k.next_state = next_section(k.mixed)
@@ -231,41 +264,36 @@
     def made(c, visit, state, rows):
         k = Chunk()
         k.state, k.rows, k.c, k.visit = state, rows, c, visit
+        k.span = spans[c] if visit == 0 else slice(0, chunk)
         return k
 
-    a = made(0, 0, states[0], rows[0])
-    gather_1(a)
-    gather_2(a)
-    gather_3(a)
-    b = made(1, 0, states[1], after(rows[1], a.across_right))
-    gather_1(b)
-    up(a)
-    down(a, b.left, b.right, b.across)
+    swapped = (up_sib, down_sib)
+    a = made(0, 0, activations[0], rows[0])
+    b = made(1, 0, activations[0], rows[1])
     for visit in range(STOPS):
-        last = visit == STOPS - 1
-        return_1(a)
+        gather_1(a)
+        gather_2(a)
+        gather_3(a)
+        if visit == 0:
+            b.rows = after(b.rows, a.left, a.right, a.across)
+        gather_1(b, ())
         gather_2(b)
         gather_3(b)
+        up(a, b.right)
+        down(a, b.pair, b.across_right)
+        return_1(a, (), ())
         return_2(a)
+        return_3(a)
         up(b, a.s_across_right)
-        return_3(a)
-        down(b, a.s_left, a.s_across, a.s_right)
-        onward(a)
-        return_1(b)
+        down(b, a.s_right)
+        return_1(b, (a.mixed,), ())
         return_2(b)
         return_3(b)
+        onward(a)
         onward(b)
-        if last:
+        if visit == STOPS - 1:
             return jnp.concatenate([a.next_state, b.next_state])[None]
-        c = made(0, visit + 1, a.next_state, a.next_rows)
-        gather_1(c)
-        gather_2(c)
-        gather_3(c)
-        d = made(1, visit + 1, b.next_state, b.next_rows)
-        gather_1(d)
-        up(c, d.rows)
-        down(c, d.left, d.right, d.across)
-        a, b = c, d
+        a, b = made(0, visit + 1, a.next_state, a.next_rows), made(1, visit + 1, b.next_state, b.next_rows)
 
 
 def solution(mesh):

time: 380 us -> 341 us (0.90)
  waiting for transfers between devices: 201 us -> 151 us
  starting transfers between devices: 81.2 us -> 94.2 us
  other arithmetic: 6.77 us -> 2.12 us
    ppermute x50, waiting for transfers between devices: 172 us -> 136 us  [send(): return lax.ppermute(value, 'expert', MOVES[way])]
    ppermute x4, waiting for transfers between devices: 29.2 us -> 14.5 us  [next_section(): lax.ppermute(value, 'section', [(s, (s + 1) % count) for s in range(count)])]
    ppermute x50, starting transfers between devices: 79 us -> 87.8 us  [send(): return lax.ppermute(value, 'expert', MOVES[way])]
    ppermute x4, starting transfers between devices: 2.16 us -> 6.38 us  [next_section(): lax.ppermute(value, 'section', [(s, (s + 1) % count) for s in range(count)])]
  transfers between devices with their start and end apart: 54 -> 54, of which waited for: 27 -> 27; matrix products, arithmetic and copies ran while one was open for 2% -> 1% of each run, Pallas kernels for 16% -> 24%
where the time goes in v2:
time: 341 us; the launch traced here: 335 us
  waiting for transfers between devices  151 us (44%)
  starting transfers between devices  94.2 us (28%)
  Pallas kernels  80.8 us (24%)
  local copies, waits for them, and re-layouts  6.56 us (2%)
    ppermute x50, waiting for transfers between devices, send(): return lax.ppermute(value, 'expert', MOVES[way])  136 us
    ppermute x50, starting transfers between devices, send(): return lax.ppermute(value, 'expert', MOVES[way])  87.8 us
    pallas_call x4, Pallas kernels, up_call(): pl.pallas_call(functools.partial(up_kernel, len(pieces)), in_specs=[WHOLE...  38.4 us
    pallas_call x4, Pallas kernels, down_call(): pl.pallas_call(down_kernel, in_specs=[WHOLE] * 3, out_specs=[WHOLE] * len...  38 us
    ppermute x4, waiting for transfers between devices, next_section(): lax.ppermute(value, 'section', [(s, (s + 1) % count) for s in range(count)])  14.5 us
  transfers between devices with their start and end apart: 54, of which 27 were waited for; matrix products, arithmetic and copies ran while one was open for 1% of the time, Pallas kernels for 24%

profile of v2, /device:TPU:0, one launch (start us, length us, event | category | flops | bytes accessed | tf_op | source)
XLA Modules:
  0.0 335.3 jit_solution(7981919879846893695)
XLA Ops:
  8.5 4.0 %collective-permute-start.2 = (bf16[64,4224]{1,0:T(8,128)(2,1)S(1)}, bf16[64,4224]{1,0:T(8,128)(2,1)S(1)}, u32[]{:S(2)}, u32[]{:S(2)}) collective-permute-start(bf16[64,4224]{1,0:T(8,128)(2,1)S(1)} %norm.5.refs_1_), channel_id=1, source_target_pairs={{0,4},{2,6},{4,0},{6,2},{8,12},{10,14},{12,8},{14,10},{16,20},{18,... | collective-permute-start | bytes 1622024 | tf_op jit(solution)/shard_map/across_0_0/ppermute | solution.py:41
  12.9 7.8 %collective-permute-done.refs_2_ = bf16[64,4224]{1,0:T(8,128)(2,1)S(1)} collective-permute-done((bf16[64,4224]{1,0:T(8,128)(2,1)S(1)}, bf16[64,4224]{1,0:T(8,128)(2,1)S(1)}, u32[]{:S(2)}, u32[]{:S(2)}) %collective-permute-start) | collective-permute-done | bytes 540704 | tf_op jit(solution)/shard_map/left_0_0/ppermute | solution.py:41
  20.7 3.6 %collective-permute-done.2.refs_4_ = bf16[64,4224]{1,0:T(8,128)(2,1)S(1)} collective-permute-done((bf16[64,4224]{1,0:T(8,128)(2,1)S(1)}, bf16[64,4224]{1,0:T(8,128)(2,1)S(1)}, u32[]{:S(2)}, u32[]{:S(2)}) %collective-permute-start.2) | collective-permute-done | bytes 540704 | tf_op jit(solution)/shard_map/across_0_0/ppermute | solution.py:41
  25.9 3.2 collective-permute-start.10
  29.7 7.7 %collective-permute-done.3.refs_3_ = bf16[64,4224]{1,0:T(8,128)(2,1)S(1)} collective-permute-done((bf16[64,4224]{1,0:T(8,128)(2,1)S(1)}, bf16[64,4224]{1,0:T(8,128)(2,1)S(1)}, u32[]{:S(2)}, u32[]{:S(2)}) %collective-permute-start.3) | collective-permute-done | bytes 540704 | tf_op jit(solution)/shard_map/right_1_0/ppermute | solution.py:41
  37.6 2.9 collective-permute-start.11
  41.2 4.4 %collective-permute-done.9.refs_2_ = bf16[64,4224]{1,0:T(8,128)(2,1)S(1)} collective-permute-done((bf16[64,4224]{1,0:T(8,128)(2,1)S(1)}, bf16[64,4224]{1,0:T(8,128)(2,1)S(1)}, u32[]{:S(2)}, u32[]{:S(2)}) %collective-permute-start.9) | collective-permute-done | bytes 540704 | tf_op jit(solution)/shard_map/left_1_0/ppermute | solution.py:41
  45.6 17.7 %collective-permute-done.7.refs_6_ = bf16[64,4224]{1,0:T(8,128)(2,1)S(1)} collective-permute-done((bf16[64,4224]{1,0:T(8,128)(2,1)S(1)}, bf16[64,4224]{1,0:T(8,128)(2,1)S(1)}, u32[]{:S(2)}, u32[]{:S(2)}) %collective-permute-start.7) | collective-permute-done | bytes 540704 | tf_op jit(solution)/shard_map/across_right_0_0/ppermute | solution.py:41
  65.7 3.5 %collective-permute-start.20 = (bf16[64,4224]{1,0:T(8,128)(2,1)S(1)}, bf16[64,4224]{1,0:T(8,128)(2,1)S(1)}, u32[]{:S(2)}, u32[]{:S(2)}) collective-permute-start(bf16[64,4224]{1,0:T(8,128)(2,1)S(1)} %collective-permute-done.11.refs_6_), channel_id=1, source_target_pairs={{0,24},{2,26},{4,28},{6,30},{8,0},{10,2},{12,4},{14,6},{16,8},{18,... | collective-permute-start | bytes 1622024 | tf_op jit(solution)/shard_map/across_far_1_0/ppermute | solution.py:41
  69.1 9.4 %collective-permute-done.8.refs_7_ = bf16[64,4224]{1,0:T(8,128)(2,1)S(1)} collective-permute-done((bf16[64,4224]{1,0:T(8,128)(2,1)S(1)}, bf16[64,4224]{1,0:T(8,128)(2,1)S(1)}, u32[]{:S(2)}, u32[]{:S(2)}) %collective-permute-start.8) | collective-permute-done | bytes 540704 | tf_op jit(solution)/shard_map/across_far_0_0/ppermute | solution.py:41
  78.5 2.8 copy-done.4
  81.3 9.7 %up.4.hidden_ref = bf16[512,1536]{1,0:T(8,128)(2,1)S(1)} custom-call(f32[2,128]{1,0:T(2,128)S(1)} %and_convert_fusion.refs_0_, bf16[64,4224]{1,0:T(8,128)(2,1)S(1)} %norm.5.refs_1_, bf16[64,4224]{1,0:T(8,128)(2,1)S(1)} %collective-permute-done.refs_2_, bf16[64,4224]{1,0:T(8,128)(2,1)S(1)} %collective-permute-done.1.refs_3_, ...), custom_call_target="tpu_custom_call" | custom-call | flops 6442450944 | bytes 18350080 | tf_op jit(solution)/shard_map/up/pallas_call | solution.py:111
  91.0 9.6 %down.4 = (bf16[64,4096]{1,0:T(8,128)(2,1)S(1)}, bf16[64,4096]{1,0:T(8,128)(2,1)S(1)}, bf16[64,4096]{1,0:T(8,128)(2,1)S(1)}, bf16[64,4096]{1,0:T(8,128)(2,1)S(1)...) custom-call(bf16[512,1536]{1,0:T(8,128)(2,1)S(1)} %up.4.hidden_ref, ...), custom_call_target="tpu_custom_call" | custom-call | flops 6442450944 | bytes 18350080 | tf_op jit(solution)/shard_map/down/pallas_call | solution.py:141
  101.8 2.4 collective-permute-start.15
  104.2 7.1 %collective-permute-done.12.b_ref = bf16[64,4096]{1,0:T(8,128)(2,1)S(1)} collective-permute-done((bf16[64,4096]{1,0:T(8,128)(2,1)S(1)}, bf16[64,4096]{1,0:T(8,128)(2,1)S(1)}, u32[]{:S(2)}, u32[]{:S(2)}) %collective-permute-start.12) | collective-permute-done | bytes 524320 | tf_op jit(solution)/shard_map/back_1_far_0_0/ppermute | solution.py:41
  111.4 3.4 %collective-permute-start.13 = (bf16[64,4096]{1,0:T(8,128)(2,1)S(1)}, bf16[64,4096]{1,0:T(8,128)(2,1)S(1)}, u32[]{:S(2)}, u32[]{:S(2)}) collective-permute-start(bf16[64,4096]{1,0:T(8,128)(2,1)S(1)} %plus.16), channel_id=1, source_target_pairs={{0,4},{2,6},{4,0},{6,2},{8,12},{10,14},{12,8},{14,10},{16,20},{18,... | collective-permute-start | bytes 1572872 | tf_op jit(solution)/shard_map/back_2_0_0/ppermute | solution.py:41
  114.7 9.6 %up.5.hidden_ref = bf16[512,1536]{1,0:T(8,128)(2,1)S(1)} custom-call(f32[2,128]{1,0:T(2,128)S(1)} %and_convert_fusion.refs_0_, bf16[64,4224]{1,0:T(8,128)(2,1)S(1)} %norm.4.refs_1_, bf16[64,4224]{1,0:T(8,128)(2,1)S(1)} %collective-permute-done.9.refs_2_, bf16[64,4224]{1,0:T(8,128)(2,1)S(1)} %collective-permute-done.3.refs_3_, ...), custom_call_target="tpu_custom_call" | custom-call | flops 6442450944 | bytes 18350080 | tf_op jit(solution)/shard_map/up/pallas_call | solution.py:111
  125.5 2.9 collective-permute-start.16
  128.5 9.4 %down.5 = (bf16[64,4096]{1,0:T(8,128)(2,1)S(1)}, bf16[64,4096]{1,0:T(8,128)(2,1)S(1)}, bf16[64,4096]{1,0:T(8,128)(2,1)S(1)}, bf16[64,4096]{1,0:T(8,128)(2,1)S(1)...) custom-call(bf16[512,1536]{1,0:T(8,128)(2,1)S(1)} %up.5.hidden_ref, ...), custom_call_target="tpu_custom_call" | custom-call | flops 6442450944 | bytes 18350080 | tf_op jit(solution)/shard_map/down/pallas_call | solution.py:141
  138.0 3.3 collective-permute-start.24
  141.3 2.5 collective-permute-done.14.refs_1_
  144.2 10.4 %collective-permute-done.21.b_ref = bf16[64,4096]{1,0:T(8,128)(2,1)S(1)} collective-permute-done((bf16[64,4096]{1,0:T(8,128)(2,1)S(1)}, bf16[64,4096]{1,0:T(8,128)(2,1)S(1)}, u32[]{:S(2)}, u32[]{:S(2)}) %collective-permute-start.21) | collective-permute-done | bytes 524320 | tf_op jit(solution)/shard_map/back_1_far_1_0/ppermute | solution.py:41
  159.0 4.2 %collective-permute-start.26 = (bf16[64,4096]{1,0:T(8,128)(2,1)S(1)}, bf16[64,4096]{1,0:T(8,128)(2,1)S(1)}, u32[]{:S(2)}, u32[]{:S(2)}) collective-permute-start(bf16[64,4096]{1,0:T(8,128)(2,1)S(1)} %plus.23), channel_id=1, source_target_pairs={{0,4},{2,6},{4,0},{6,2},{8,12},{10,14},{12,8},{14,10},{16,20},{18,... | collective-permute-start | bytes 1572872 | tf_op jit(solution)/shard_map/back_3_across_1_0/ppermute | solution.py:41
  167.0 3.2 collective-permute-start.30
  170.2 6.2 %collective-permute-done.26.refs_3_ = bf16[64,4096]{1,0:T(8,128)(2,1)S(1)} collective-permute-done((bf16[64,4096]{1,0:T(8,128)(2,1)S(1)}, bf16[64,4096]{1,0:T(8,128)(2,1)S(1)}, u32[]{:S(2)}, u32[]{:S(2)}) %collective-permute-start.26) | collective-permute-done | bytes 524320 | tf_op jit(solution)/shard_map/back_3_across_1_0/ppermute | solution.py:41
  176.4 3.2 collective-permute-start.31
  181.6 3.8 %collective-permute-start.33 = (bf16[64,4224]{1,0:T(8,128)(2,1)S(1)}, bf16[64,4224]{1,0:T(8,128)(2,1)S(1)}, u32[]{:S(2)}, u32[]{:S(2)}) collective-permute-start(bf16[64,4224]{1,0:T(8,128)(2,1)S(1)} %collective-permute-done.30.refs_3_), channel_id=1, source_target_pairs={{0,4},{2,6},{4,0},{6,2},{8,12},{10,14},{12,8},{14,10},{16,20},{18,... | collective-permute-start | bytes 1622024 | tf_op jit(solution)/shard_map/across_right_0_1/ppermute | solution.py:41
  185.4 5.0 %collective-permute-done.27.state_ref = bf16[64,4096]{1,0:T(8,128)(2,1)S(1)} collective-permute-done((bf16[64,4096]{1,0:T(8,128)(2,1)S(1)}, bf16[64,4096]{1,0:T(8,128)(2,1)S(1)}, u32[]{:S(2)}, u32[]{:S(2)}) %collective-permute-start.27) | collective-permute-done | bytes 524320 | tf_op jit(solution)/shard_map/ppermute | solution.py:46
  193.0 3.5 %collective-permute-done.33.refs_6_ = bf16[64,4224]{1,0:T(8,128)(2,1)S(1)} collective-permute-done((bf16[64,4224]{1,0:T(8,128)(2,1)S(1)}, bf16[64,4224]{1,0:T(8,128)(2,1)S(1)}, u32[]{:S(2)}, u32[]{:S(2)}) %collective-permute-start.33) | collective-permute-done | bytes 540704 | tf_op jit(solution)/shard_map/across_right_0_1/ppermute | solution.py:41
  196.5 5.1 %collective-permute-start.34 = (bf16[64,4224]{1,0:T(8,128)(2,1)S(1)}, bf16[64,4224]{1,0:T(8,128)(2,1)S(1)}, u32[]{:S(2)}, u32[]{:S(2)}) collective-permute-start(bf16[64,4224]{1,0:T(8,128)(2,1)S(1)} %collective-permute-done.33.refs_6_), channel_id=1, source_target_pairs={{0,24},{2,26},{4,28},{6,30},{8,0},{10,2},{12,4},{14,6},{16,8},{18,... | collective-permute-start | bytes 1622024 | tf_op jit(solution)/shard_map/across_far_0_1/ppermute | solution.py:41
  201.6 2.6 collective-permute-start.36
  204.2 3.4 collective-permute-done.35.refs_2_
  207.6 9.0 %collective-permute-done.36.refs_4_ = bf16[64,4224]{1,0:T(8,128)(2,1)S(1)} collective-permute-done((bf16[64,4224]{1,0:T(8,128)(2,1)S(1)}, bf16[64,4224]{1,0:T(8,128)(2,1)S(1)}, u32[]{:S(2)}, u32[]{:S(2)}) %collective-permute-start.36) | collective-permute-done | bytes 540704 | tf_op jit(solution)/shard_map/across_1_1/ppermute | solution.py:41
  216.8 3.3 collective-permute-start.37
  220.1 9.3 %collective-permute-done.32.refs_5_ = bf16[128,4224]{1,0:T(8,128)(2,1)S(1)} collective-permute-done((bf16[128,4224]{1,0:T(8,128)(2,1)S(1)}, bf16[128,4224]{1,0:T(8,128)(2,1)S(1)}, u32[]{:S(2)}, u32[]{:S(2)}) %collective-permute-start.32) | collective-permute-done | bytes 1081376 | tf_op jit(solution)/shard_map/far_and_left_0_1/ppermute | solution.py:41
  229.4 9.6 %up.6.hidden_ref = bf16[512,1536]{1,0:T(8,128)(2,1)S(1)} custom-call(f32[2,128]{1,0:T(2,128)S(1)} %and_convert_fusion.refs_0_, bf16[64,4224]{1,0:T(8,128)(2,1)S(1)} %norm.7.refs_1_, bf16[64,4224]{1,0:T(8,128)(2,1)S(1)} %collective-permute-done.29.refs_2_, bf16[64,4224]{1,0:T(8,128)(2,1)S(1)} %collective-permute-done.30.refs_3_, ...), custom_call_target="tpu_custom_call" | custom-call | flops 6442450944 | bytes 18350080 | tf_op jit(solution)/shard_map/up/pallas_call | solution.py:111
  239.7 9.4 %down.6 = (bf16[64,4096]{1,0:T(8,128)(2,1)S(1)}, bf16[64,4096]{1,0:T(8,128)(2,1)S(1)}, bf16[64,4096]{1,0:T(8,128)(2,1)S(1)}, bf16[64,4096]{1,0:T(8,128)(2,1)S(1)...) custom-call(bf16[512,1536]{1,0:T(8,128)(2,1)S(1)} %up.6.hidden_ref, ...), custom_call_target="tpu_custom_call" | custom-call | flops 6442450944 | bytes 18350080 | tf_op jit(solution)/shard_map/down/pallas_call | solution.py:141
  252.4 7.2 %collective-permute-done.38.b_ref = bf16[64,4096]{1,0:T(8,128)(2,1)S(1)} collective-permute-done((bf16[64,4096]{1,0:T(8,128)(2,1)S(1)}, bf16[64,4096]{1,0:T(8,128)(2,1)S(1)}, u32[]{:S(2)}, u32[]{:S(2)}) %collective-permute-start.38) | collective-permute-done | bytes 524320 | tf_op jit(solution)/shard_map/back_1_far_0_1/ppermute | solution.py:41
  259.7 3.1 collective-permute-start.39
  262.8 9.6 %up.7.hidden_ref = bf16[512,1536]{1,0:T(8,128)(2,1)S(1)} custom-call(f32[2,128]{1,0:T(2,128)S(1)} %and_convert_fusion.refs_0_, bf16[64,4224]{1,0:T(8,128)(2,1)S(1)} %norm.6.refs_1_, bf16[64,4224]{1,0:T(8,128)(2,1)S(1)} %collective-permute-done.35.refs_2_, bf16[64,4224]{1,0:T(8,128)(2,1)S(1)} %collective-permute-done.28.refs_3_, ...), custom_call_target="tpu_custom_call" | custom-call | flops 6442450944 | bytes 18350080 | tf_op jit(solution)/shard_map/up/pallas_call | solution.py:111
  272.6 2.5 collective-permute-start.40
  277.6 9.6 %down.7 = (bf16[64,4096]{1,0:T(8,128)(2,1)S(1)}, bf16[64,4096]{1,0:T(8,128)(2,1)S(1)}, bf16[64,4096]{1,0:T(8,128)(2,1)S(1)}, bf16[64,4096]{1,0:T(8,128)(2,1)S(1)...) custom-call(bf16[512,1536]{1,0:T(8,128)(2,1)S(1)} %up.7.hidden_ref, ...), custom_call_target="tpu_custom_call" | custom-call | flops 6442450944 | bytes 18350080 | tf_op jit(solution)/shard_map/down/pallas_call | solution.py:141
  289.6 10.8 %collective-permute-done.47.b_ref = bf16[64,4096]{1,0:T(8,128)(2,1)S(1)} collective-permute-done((bf16[64,4096]{1,0:T(8,128)(2,1)S(1)}, bf16[64,4096]{1,0:T(8,128)(2,1)S(1)}, u32[]{:S(2)}, u32[]{:S(2)}) %collective-permute-start.47) | collective-permute-done | bytes 524320 | tf_op jit(solution)/shard_map/back_1_far_1_1/ppermute | solution.py:41
  302.7 4.9 %collective-permute-done.50.b_ref = bf16[128,4096]{1,0:T(8,128)(2,1)S(1)} collective-permute-done((bf16[128,4096]{1,0:T(8,128)(2,1)S(1)}, bf16[128,4096]{1,0:T(8,128)(2,1)S(1)}, u32[]{:S(2)}, u32[]{:S(2)}) %collective-permute-start.50) | collective-permute-done | bytes 1048608 | tf_op jit(solution)/shard_map/back_1_both_1_1/ppermute | solution.py:41
  307.7 2.6 collective-permute-start.52
  314.7 3.8 %collective-permute-done.52.refs_3_ = bf16[64,4096]{1,0:T(8,128)(2,1)S(1)} collective-permute-done((bf16[64,4096]{1,0:T(8,128)(2,1)S(1)}, bf16[64,4096]{1,0:T(8,128)(2,1)S(1)}, u32[]{:S(2)}, u32[]{:S(2)}) %collective-permute-start.52) | collective-permute-done | bytes 524320 | tf_op jit(solution)/shard_map/back_3_across_1_1/ppermute | solution.py:41
  319.7 3.5 %collective-permute-done.49.refs_1_ = bf16[64,4096]{1,0:T(8,128)(2,1)S(1)} collective-permute-done((bf16[64,4096]{1,0:T(8,128)(2,1)S(1)}, bf16[64,4096]{1,0:T(8,128)(2,1)S(1)}, u32[]{:S(2)}, u32[]{:S(2)}) %collective-permute-start.49) | collective-permute-done | bytes 524320 | tf_op jit(solution)/shard_map/back_3_right_1_1/ppermute | solution.py:41
  324.9 9.2 %collective-permute-done.53 = bf16[64,4096]{1,0:T(8,128)(2,1)S(1)} collective-permute-done((bf16[64,4096]{1,0:T(8,128)(2,1)S(1)}, bf16[64,4096]{1,0:T(8,128)(2,1)S(1)}, u32[]{:S(2)}, u32[]{:S(2)}) %collective-permute-start.53) | collective-permute-done | bytes 524320 | tf_op jit(solution)/shard_map/ppermute | solution.py:46
  (125 shorter events, 50.0 us)
Async XLA Ops:
  0.0 37.6 %collective-permute-start.5 = (bf16[4096,768]{1,0:T(8,128)(2,1)}, bf16[4096,768]{1,0:T(8,128)(2,1)}, u32[]{:S(2)}, u32[]{:S(2)}) collective-permute-start(bf16[4096,768]{1,0:T(8,128)(2,1)} %bitcast.13), channel_id=1, source_target_pairs={{0,2},{2,0},{4,6},{6,4},{8,10},{10,8},{12,14},{14,12},{16,18},{18,... | collective-permute-start | bytes 18874376 | tf_op jit(solution)/shard_map/sibling/ppermute | solution.py:41
  0.0 40.6 %collective-permute-start.6 = (bf16[768,4096]{1,0:T(8,128)(2,1)}, bf16[768,4096]{1,0:T(8,128)(2,1)}, u32[]{:S(2)}, u32[]{:S(2)}) collective-permute-start(bf16[768,4096]{1,0:T(8,128)(2,1)} %bitcast.20), channel_id=1, source_target_pairs={{0,2},{2,0},{4,6},{6,4},{8,10},{10,8},{12,14},{14,12},{16,18},{18,... | collective-permute-start | bytes 18874376 | tf_op jit(solution)/shard_map/sibling/ppermute | solution.py:41
  5.2 15.5 %collective-permute-start = (bf16[64,4224]{1,0:T(8,128)(2,1)S(1)}, bf16[64,4224]{1,0:T(8,128)(2,1)S(1)}, u32[]{:S(2)}, u32[]{:S(2)}) collective-permute-start(bf16[64,4224]{1,0:T(8,128)(2,1)S(1)} %norm.5.refs_1_), channel_id=1, source_target_pairs={{0,8},{2,10},{4,12},{6,14},{8,16},{10,18},{12,20},{14,22},{16,24},... | collective-permute-start | bytes 1622024 | tf_op jit(solution)/shard_map/left_0_0/ppermute | solution.py:41
  6.8 13.9 %collective-permute-start.1 = (bf16[64,4224]{1,0:T(8,128)(2,1)S(1)}, bf16[64,4224]{1,0:T(8,128)(2,1)S(1)}, u32[]{:S(2)}, u32[]{:S(2)}) collective-permute-start(bf16[64,4224]{1,0:T(8,128)(2,1)S(1)} %norm.5.refs_1_), channel_id=1, source_target_pairs={{0,24},{2,26},{4,28},{6,30},{8,0},{10,2},{12,4},{14,6},{16,8},{18,... | collective-permute-start | bytes 1622024 | tf_op jit(solution)/shard_map/right_0_0/ppermute | solution.py:41
  8.5 15.8 %collective-permute-start.2 = (bf16[64,4224]{1,0:T(8,128)(2,1)S(1)}, bf16[64,4224]{1,0:T(8,128)(2,1)S(1)}, u32[]{:S(2)}, u32[]{:S(2)}) collective-permute-start(bf16[64,4224]{1,0:T(8,128)(2,1)S(1)} %norm.5.refs_1_), channel_id=1, source_target_pairs={{0,4},{2,6},{4,0},{6,2},{8,12},{10,14},{12,8},{14,10},{16,20},{18,... | collective-permute-start | bytes 1622024 | tf_op jit(solution)/shard_map/across_0_0/ppermute | solution.py:41
  24.3 13.0 %collective-permute-start.3 = (bf16[64,4224]{1,0:T(8,128)(2,1)S(1)}, bf16[64,4224]{1,0:T(8,128)(2,1)S(1)}, u32[]{:S(2)}, u32[]{:S(2)}) collective-permute-start(bf16[64,4224]{1,0:T(8,128)(2,1)S(1)} %norm.4.refs_1_), channel_id=1, source_target_pairs={{0,24},{2,26},{4,28},{6,30},{8,0},{10,2},{12,4},{14,6},{16,8},{18,... | collective-permute-start | bytes 1622024 | tf_op jit(solution)/shard_map/right_1_0/ppermute | solution.py:41
  25.9 39.6 %collective-permute-start.10 = (bf16[64,4224]{1,0:T(8,128)(2,1)S(1)}, bf16[64,4224]{1,0:T(8,128)(2,1)S(1)}, u32[]{:S(2)}, u32[]{:S(2)}) collective-permute-start(bf16[64,4224]{1,0:T(8,128)(2,1)S(1)} %norm.4.refs_1_), channel_id=1, source_target_pairs={{0,4},{2,6},{4,0},{6,2},{8,12},{10,14},{12,8},{14,10},{16,20},{18,... | collective-permute-start | bytes 1622024 | tf_op jit(solution)/shard_map/across_1_0/ppermute | solution.py:41
  29.1 16.4 %collective-permute-start.9 = (bf16[64,4224]{1,0:T(8,128)(2,1)S(1)}, bf16[64,4224]{1,0:T(8,128)(2,1)S(1)}, u32[]{:S(2)}, u32[]{:S(2)}) collective-permute-start(bf16[64,4224]{1,0:T(8,128)(2,1)S(1)} %norm.4.refs_1_), channel_id=1, source_target_pairs={{0,8},{2,10},{4,12},{6,14},{8,16},{10,18},{12,20},{14,22},{16,24},... | collective-permute-start | bytes 1622024 | tf_op jit(solution)/shard_map/left_1_0/ppermute | solution.py:41
  37.4 31.8 %collective-permute-start.4 = (bf16[128,4224]{1,0:T(8,128)(2,1)S(1)}, bf16[128,4224]{1,0:T(8,128)(2,1)S(1)}, u32[]{:S(2)}, u32[]{:S(2)}) collective-permute-start(bf16[128,4224]{1,0:T(8,128)(2,1)S(1)} %pad_maximum_fusion), channel_id=1, source_target_pairs={{0,8},{2,10},{4,12},{6,14},{8,16},{10,18},{12,20},{14,22},{16,24},... | collective-permute-start | bytes 3244040 | tf_op jit(solution)/shard_map/far_and_left_0_0/ppermute | solution.py:41
  37.6 28.0 %collective-permute-start.11 = (bf16[64,4224]{1,0:T(8,128)(2,1)S(1)}, bf16[64,4224]{1,0:T(8,128)(2,1)S(1)}, u32[]{:S(2)}, u32[]{:S(2)}) collective-permute-start(bf16[64,4224]{1,0:T(8,128)(2,1)S(1)} %collective-permute-done.3.refs_3_), channel_id=1, source_target_pairs={{0,4},{2,6},{4,0},{6,2},{8,12},{10,14},{12,8},{14,10},{16,20},{18,... | collective-permute-start | bytes 1622024 | tf_op jit(solution)/shard_map/across_right_1_0/ppermute | solution.py:41
  40.6 22.7 %collective-permute-start.7 = (bf16[64,4224]{1,0:T(8,128)(2,1)S(1)}, bf16[64,4224]{1,0:T(8,128)(2,1)S(1)}, u32[]{:S(2)}, u32[]{:S(2)}) collective-permute-start(bf16[64,4224]{1,0:T(8,128)(2,1)S(1)} %collective-permute-done.1.refs_3_), channel_id=1, source_target_pairs={{0,4},{2,6},{4,0},{6,2},{8,12},{10,14},{12,8},{14,10},{16,20},{18,... | collective-permute-start | bytes 1622024 | tf_op jit(solution)/shard_map/across_right_0_0/ppermute | solution.py:41
  63.3 15.2 %collective-permute-start.8 = (bf16[64,4224]{1,0:T(8,128)(2,1)S(1)}, bf16[64,4224]{1,0:T(8,128)(2,1)S(1)}, u32[]{:S(2)}, u32[]{:S(2)}) collective-permute-start(bf16[64,4224]{1,0:T(8,128)(2,1)S(1)} %collective-permute-done.7.refs_6_), channel_id=1, source_target_pairs={{0,24},{2,26},{4,28},{6,30},{8,0},{10,2},{12,4},{14,6},{16,8},{18,... | collective-permute-start | bytes 1622024 | tf_op jit(solution)/shard_map/across_far_0_0/ppermute | solution.py:41
  65.6 49.2 %collective-permute-start.19 = (bf16[128,4224]{1,0:T(8,128)(2,1)S(1)}, bf16[128,4224]{1,0:T(8,128)(2,1)S(1)}, u32[]{:S(2)}, u32[]{:S(2)}) collective-permute-start(bf16[128,4224]{1,0:T(8,128)(2,1)S(1)} %constant_dynamic-update-slice_fusion), channel_id=1, source_target_pairs={{0,8},{2,10},{4,12},{6,14},{8,16},{10,18},{12,20},{14,22},{16,24},... | collective-permute-start | bytes 3244040 | tf_op jit(solution)/shard_map/far_and_left_1_0/ppermute | solution.py:41
  65.7 49.1 %collective-permute-start.20 = (bf16[64,4224]{1,0:T(8,128)(2,1)S(1)}, bf16[64,4224]{1,0:T(8,128)(2,1)S(1)}, u32[]{:S(2)}, u32[]{:S(2)}) collective-permute-start(bf16[64,4224]{1,0:T(8,128)(2,1)S(1)} %collective-permute-done.11.refs_6_), channel_id=1, source_target_pairs={{0,24},{2,26},{4,28},{6,30},{8,0},{10,2},{12,4},{14,6},{16,8},{18,... | collective-permute-start | bytes 1622024 | tf_op jit(solution)/shard_map/across_far_1_0/ppermute | solution.py:41
  100.6 10.6 %collective-permute-start.12 = (bf16[64,4096]{1,0:T(8,128)(2,1)S(1)}, bf16[64,4096]{1,0:T(8,128)(2,1)S(1)}, u32[]{:S(2)}, u32[]{:S(2)}) collective-permute-start(bf16[64,4096]{1,0:T(8,128)(2,1)S(1)} %get-tuple-element.52), channel_id=1, source_target_pairs={{0,8},{2,10},{4,12},{6,14},{8,16},{10,18},{12,20},{14,22},{16,24},... | collective-permute-start | bytes 1572872 | tf_op jit(solution)/shard_map/back_1_far_0_0/ppermute | solution.py:41
  101.8 22.6 %collective-permute-start.15 = (bf16[128,4096]{1,0:T(8,128)(2,1)S(1)}, bf16[128,4096]{1,0:T(8,128)(2,1)S(1)}, u32[]{:S(2)}, u32[]{:S(2)}) collective-permute-start(bf16[128,4096]{1,0:T(8,128)(2,1)S(1)} %get-tuple-element.54), channel_id=1, source_target_pairs={{0,24},{2,26},{4,28},{6,30},{8,0},{10,2},{12,4},{14,6},{16,8},{18,... | collective-permute-start | bytes 3145736 | tf_op jit(solution)/shard_map/back_1_both_0_0/ppermute | solution.py:41
  111.4 17.0 %collective-permute-start.13 = (bf16[64,4096]{1,0:T(8,128)(2,1)S(1)}, bf16[64,4096]{1,0:T(8,128)(2,1)S(1)}, u32[]{:S(2)}, u32[]{:S(2)}) collective-permute-start(bf16[64,4096]{1,0:T(8,128)(2,1)S(1)} %plus.16), channel_id=1, source_target_pairs={{0,4},{2,6},{4,0},{6,2},{8,12},{10,14},{12,8},{14,10},{16,20},{18,... | collective-permute-start | bytes 1572872 | tf_op jit(solution)/shard_map/back_2_0_0/ppermute | solution.py:41
  124.5 16.8 %collective-permute-start.17 = (bf16[64,4096]{1,0:T(8,128)(2,1)S(1)}, bf16[64,4096]{1,0:T(8,128)(2,1)S(1)}, u32[]{:S(2)}, u32[]{:S(2)}) collective-permute-start(bf16[64,4096]{1,0:T(8,128)(2,1)S(1)} %plus.19), channel_id=1, source_target_pairs={{0,4},{2,6},{4,0},{6,2},{8,12},{10,14},{12,8},{14,10},{16,20},{18,... | collective-permute-start | bytes 1572872 | tf_op jit(solution)/shard_map/back_3_across_0_0/ppermute | solution.py:41
  125.5 15.8 %collective-permute-start.16 = (bf16[64,4096]{1,0:T(8,128)(2,1)S(1)}, bf16[64,4096]{1,0:T(8,128)(2,1)S(1)}, u32[]{:S(2)}, u32[]{:S(2)}) collective-permute-start(bf16[64,4096]{1,0:T(8,128)(2,1)S(1)} %plus.18), channel_id=1, source_target_pairs={{0,24},{2,26},{4,28},{6,30},{8,0},{10,2},{12,4},{14,6},{16,8},{18,... | collective-permute-start | bytes 1572872 | tf_op jit(solution)/shard_map/back_3_left_0_0/ppermute | solution.py:41
  128.4 15.3 %collective-permute-start.14 = (bf16[64,4096]{1,0:T(8,128)(2,1)S(1)}, bf16[64,4096]{1,0:T(8,128)(2,1)S(1)}, u32[]{:S(2)}, u32[]{:S(2)}) collective-permute-start(bf16[64,4096]{1,0:T(8,128)(2,1)S(1)} %plus.17), channel_id=1, source_target_pairs={{0,8},{2,10},{4,12},{6,14},{8,16},{10,18},{12,20},{14,22},{16,24},... | collective-permute-start | bytes 1572872 | tf_op jit(solution)/shard_map/back_3_right_0_0/ppermute | solution.py:41
  138.0 20.9 %collective-permute-start.24 = (bf16[128,4096]{1,0:T(8,128)(2,1)S(1)}, bf16[128,4096]{1,0:T(8,128)(2,1)S(1)}, u32[]{:S(2)}, u32[]{:S(2)}) collective-permute-start(bf16[128,4096]{1,0:T(8,128)(2,1)S(1)} %get-tuple-element.64), channel_id=1, source_target_pairs={{0,24},{2,26},{4,28},{6,30},{8,0},{10,2},{12,4},{14,6},{16,8},{18,... | collective-permute-start | bytes 3145736 | tf_op jit(solution)/shard_map/back_1_both_1_0/ppermute | solution.py:41
  154.7 11.3 %collective-permute-start.22 = (bf16[64,4096]{1,0:T(8,128)(2,1)S(1)}, bf16[64,4096]{1,0:T(8,128)(2,1)S(1)}, u32[]{:S(2)}, u32[]{:S(2)}) collective-permute-start(bf16[64,4096]{1,0:T(8,128)(2,1)S(1)} %plus.20), channel_id=1, source_target_pairs={{0,4},{2,6},{4,0},{6,2},{8,12},{10,14},{12,8},{14,10},{16,20},{18,... | collective-permute-start | bytes 1572872 | tf_op jit(solution)/shard_map/back_2_1_0/ppermute | solution.py:41
  159.0 17.4 %collective-permute-start.26 = (bf16[64,4096]{1,0:T(8,128)(2,1)S(1)}, bf16[64,4096]{1,0:T(8,128)(2,1)S(1)}, u32[]{:S(2)}, u32[]{:S(2)}) collective-permute-start(bf16[64,4096]{1,0:T(8,128)(2,1)S(1)} %plus.23), channel_id=1, source_target_pairs={{0,4},{2,6},{4,0},{6,2},{8,12},{10,14},{12,8},{14,10},{16,20},{18,... | collective-permute-start | bytes 1572872 | tf_op jit(solution)/shard_map/back_3_across_1_0/ppermute | solution.py:41
  163.4 16.3 %collective-permute-start.25 = (bf16[64,4096]{1,0:T(8,128)(2,1)S(1)}, bf16[64,4096]{1,0:T(8,128)(2,1)S(1)}, u32[]{:S(2)}, u32[]{:S(2)}) collective-permute-start(bf16[64,4096]{1,0:T(8,128)(2,1)S(1)} %plus.22), channel_id=1, source_target_pairs={{0,24},{2,26},{4,28},{6,30},{8,0},{10,2},{12,4},{14,6},{16,8},{18,... | collective-permute-start | bytes 1572872 | tf_op jit(solution)/shard_map/back_3_left_1_0/ppermute | solution.py:41
  166.2 13.5 %collective-permute-start.23 = (bf16[64,4096]{1,0:T(8,128)(2,1)S(1)}, bf16[64,4096]{1,0:T(8,128)(2,1)S(1)}, u32[]{:S(2)}, u32[]{:S(2)}) collective-permute-start(bf16[64,4096]{1,0:T(8,128)(2,1)S(1)} %plus.21), channel_id=1, source_target_pairs={{0,8},{2,10},{4,12},{6,14},{8,16},{10,18},{12,20},{14,22},{16,24},... | collective-permute-start | bytes 1572872 | tf_op jit(solution)/shard_map/back_3_right_1_0/ppermute | solution.py:41
  167.0 14.6 %collective-permute-start.30 = (bf16[64,4224]{1,0:T(8,128)(2,1)S(1)}, bf16[64,4224]{1,0:T(8,128)(2,1)S(1)}, u32[]{:S(2)}, u32[]{:S(2)}) collective-permute-start(bf16[64,4224]{1,0:T(8,128)(2,1)S(1)} %norm.7.refs_1_), channel_id=1, source_target_pairs={{0,24},{2,26},{4,28},{6,30},{8,0},{10,2},{12,4},{14,6},{16,8},{18,... | collective-permute-start | bytes 1622024 | tf_op jit(solution)/shard_map/right_0_1/ppermute | solution.py:41
  170.2 22.6 %collective-permute-start.29 = (bf16[64,4224]{1,0:T(8,128)(2,1)S(1)}, bf16[64,4224]{1,0:T(8,128)(2,1)S(1)}, u32[]{:S(2)}, u32[]{:S(2)}) collective-permute-start(bf16[64,4224]{1,0:T(8,128)(2,1)S(1)} %norm.7.refs_1_), channel_id=1, source_target_pairs={{0,8},{2,10},{4,12},{6,14},{8,16},{10,18},{12,20},{14,22},{16,24},... | collective-permute-start | bytes 1622024 | tf_op jit(solution)/shard_map/left_0_1/ppermute | solution.py:41
  176.4 16.4 %collective-permute-start.31 = (bf16[64,4224]{1,0:T(8,128)(2,1)S(1)}, bf16[64,4224]{1,0:T(8,128)(2,1)S(1)}, u32[]{:S(2)}, u32[]{:S(2)}) collective-permute-start(bf16[64,4224]{1,0:T(8,128)(2,1)S(1)} %norm.7.refs_1_), channel_id=1, source_target_pairs={{0,4},{2,6},{4,0},{6,2},{8,12},{10,14},{12,8},{14,10},{16,20},{18,... | collective-permute-start | bytes 1622024 | tf_op jit(solution)/shard_map/across_0_1/ppermute | solution.py:41
  181.6 14.9 %collective-permute-start.33 = (bf16[64,4224]{1,0:T(8,128)(2,1)S(1)}, bf16[64,4224]{1,0:T(8,128)(2,1)S(1)}, u32[]{:S(2)}, u32[]{:S(2)}) collective-permute-start(bf16[64,4224]{1,0:T(8,128)(2,1)S(1)} %collective-permute-done.30.refs_3_), channel_id=1, source_target_pairs={{0,4},{2,6},{4,0},{6,2},{8,12},{10,14},{12,8},{14,10},{16,20},{18,... | collective-permute-start | bytes 1622024 | tf_op jit(solution)/shard_map/across_right_0_1/ppermute | solution.py:41
  190.7 13.5 %collective-permute-start.28 = (bf16[64,4224]{1,0:T(8,128)(2,1)S(1)}, bf16[64,4224]{1,0:T(8,128)(2,1)S(1)}, u32[]{:S(2)}, u32[]{:S(2)}) collective-permute-start(bf16[64,4224]{1,0:T(8,128)(2,1)S(1)} %norm.6.refs_1_), channel_id=1, source_target_pairs={{0,24},{2,26},{4,28},{6,30},{8,0},{10,2},{12,4},{14,6},{16,8},{18,... | collective-permute-start | bytes 1622024 | tf_op jit(solution)/shard_map/right_1_1/ppermute | solution.py:41
  191.3 16.2 %collective-permute-start.35 = (bf16[64,4224]{1,0:T(8,128)(2,1)S(1)}, bf16[64,4224]{1,0:T(8,128)(2,1)S(1)}, u32[]{:S(2)}, u32[]{:S(2)}) collective-permute-start(bf16[64,4224]{1,0:T(8,128)(2,1)S(1)} %norm.6.refs_1_), channel_id=1, source_target_pairs={{0,8},{2,10},{4,12},{6,14},{8,16},{10,18},{12,20},{14,22},{16,24},... | collective-permute-start | bytes 1622024 | tf_op jit(solution)/shard_map/left_1_1/ppermute | solution.py:41
  192.9 36.5 %collective-permute-start.32 = (bf16[128,4224]{1,0:T(8,128)(2,1)S(1)}, bf16[128,4224]{1,0:T(8,128)(2,1)S(1)}, u32[]{:S(2)}, u32[]{:S(2)}) collective-permute-start(bf16[128,4224]{1,0:T(8,128)(2,1)S(1)} %pad_maximum_fusion.1), channel_id=1, source_target_pairs={{0,8},{2,10},{4,12},{6,14},{8,16},{10,18},{12,20},{14,22},{16,24},... | collective-permute-start | bytes 3244040 | tf_op jit(solution)/shard_map/far_and_left_0_1/ppermute | solution.py:41
  196.5 32.9 %collective-permute-start.34 = (bf16[64,4224]{1,0:T(8,128)(2,1)S(1)}, bf16[64,4224]{1,0:T(8,128)(2,1)S(1)}, u32[]{:S(2)}, u32[]{:S(2)}) collective-permute-start(bf16[64,4224]{1,0:T(8,128)(2,1)S(1)} %collective-permute-done.33.refs_6_), channel_id=1, source_target_pairs={{0,24},{2,26},{4,28},{6,30},{8,0},{10,2},{12,4},{14,6},{16,8},{18,... | collective-permute-start | bytes 1622024 | tf_op jit(solution)/shard_map/across_far_0_1/ppermute | solution.py:41
  201.6 15.0 %collective-permute-start.36 = (bf16[64,4224]{1,0:T(8,128)(2,1)S(1)}, bf16[64,4224]{1,0:T(8,128)(2,1)S(1)}, u32[]{:S(2)}, u32[]{:S(2)}) collective-permute-start(bf16[64,4224]{1,0:T(8,128)(2,1)S(1)} %norm.6.refs_1_), channel_id=1, source_target_pairs={{0,4},{2,6},{4,0},{6,2},{8,12},{10,14},{12,8},{14,10},{16,20},{18,... | collective-permute-start | bytes 1622024 | tf_op jit(solution)/shard_map/across_1_1/ppermute | solution.py:41
  216.7 46.1 %collective-permute-start.45 = (bf16[128,4224]{1,0:T(8,128)(2,1)S(1)}, bf16[128,4224]{1,0:T(8,128)(2,1)S(1)}, u32[]{:S(2)}, u32[]{:S(2)}) collective-permute-start(bf16[128,4224]{1,0:T(8,128)(2,1)S(1)} %constant_dynamic-update-slice_fusion.2), channel_id=1, source_target_pairs={{0,8},{2,10},{4,12},{6,14},{8,16},{10,18},{12,20},{14,22},{16,24},... | collective-permute-start | bytes 3244040 | tf_op jit(solution)/shard_map/far_and_left_1_1/ppermute | solution.py:41
  216.8 22.2 %collective-permute-start.37 = (bf16[64,4224]{1,0:T(8,128)(2,1)S(1)}, bf16[64,4224]{1,0:T(8,128)(2,1)S(1)}, u32[]{:S(2)}, u32[]{:S(2)}) collective-permute-start(bf16[64,4224]{1,0:T(8,128)(2,1)S(1)} %collective-permute-done.28.refs_3_), channel_id=1, source_target_pairs={{0,4},{2,6},{4,0},{6,2},{8,12},{10,14},{12,8},{14,10},{16,20},{18,... | collective-permute-start | bytes 1622024 | tf_op jit(solution)/shard_map/across_right_1_1/ppermute | solution.py:41
  239.0 23.8 %collective-permute-start.46 = (bf16[64,4224]{1,0:T(8,128)(2,1)S(1)}, bf16[64,4224]{1,0:T(8,128)(2,1)S(1)}, u32[]{:S(2)}, u32[]{:S(2)}) collective-permute-start(bf16[64,4224]{1,0:T(8,128)(2,1)S(1)} %collective-permute-done.37.refs_6_), channel_id=1, source_target_pairs={{0,24},{2,26},{4,28},{6,30},{8,0},{10,2},{12,4},{14,6},{16,8},{18,... | collective-permute-start | bytes 1622024 | tf_op jit(solution)/shard_map/across_far_1_1/ppermute | solution.py:41
  250.8 24.3 %collective-permute-start.41 = (bf16[128,4096]{1,0:T(8,128)(2,1)S(1)}, bf16[128,4096]{1,0:T(8,128)(2,1)S(1)}, u32[]{:S(2)}, u32[]{:S(2)}) collective-permute-start(bf16[128,4096]{1,0:T(8,128)(2,1)S(1)} %get-tuple-element.73), channel_id=1, source_target_pairs={{0,24},{2,26},{4,28},{6,30},{8,0},{10,2},{12,4},{14,6},{16,8},{18,... | collective-permute-start | bytes 3145736 | tf_op jit(solution)/shard_map/back_1_both_0_1/ppermute | solution.py:41
  259.7 12.7 %collective-permute-start.39 = (bf16[64,4096]{1,0:T(8,128)(2,1)S(1)}, bf16[64,4096]{1,0:T(8,128)(2,1)S(1)}, u32[]{:S(2)}, u32[]{:S(2)}) collective-permute-start(bf16[64,4096]{1,0:T(8,128)(2,1)S(1)} %plus.24), channel_id=1, source_target_pairs={{0,4},{2,6},{4,0},{6,2},{8,12},{10,14},{12,8},{14,10},{16,20},{18,... | collective-permute-start | bytes 1572872 | tf_op jit(solution)/shard_map/back_2_0_1/ppermute | solution.py:41
  272.6 16.5 %collective-permute-start.40 = (bf16[64,4096]{1,0:T(8,128)(2,1)S(1)}, bf16[64,4096]{1,0:T(8,128)(2,1)S(1)}, u32[]{:S(2)}, u32[]{:S(2)}) collective-permute-start(bf16[64,4096]{1,0:T(8,128)(2,1)S(1)} %plus.25), channel_id=1, source_target_pairs={{0,8},{2,10},{4,12},{6,14},{8,16},{10,18},{12,20},{14,22},{16,24},... | collective-permute-start | bytes 1572872 | tf_op jit(solution)/shard_map/back_3_right_0_1/ppermute | solution.py:41
  275.2 12.8 %collective-permute-start.43 = (bf16[64,4096]{1,0:T(8,128)(2,1)S(1)}, bf16[64,4096]{1,0:T(8,128)(2,1)S(1)}, u32[]{:S(2)}, u32[]{:S(2)}) collective-permute-start(bf16[64,4096]{1,0:T(8,128)(2,1)S(1)} %plus.27), channel_id=1, source_target_pairs={{0,4},{2,6},{4,0},{6,2},{8,12},{10,14},{12,8},{14,10},{16,20},{18,... | collective-permute-start | bytes 1572872 | tf_op jit(solution)/shard_map/back_3_across_0_1/ppermute | solution.py:41
  276.5 12.6 %collective-permute-start.42 = (bf16[64,4096]{1,0:T(8,128)(2,1)S(1)}, bf16[64,4096]{1,0:T(8,128)(2,1)S(1)}, u32[]{:S(2)}, u32[]{:S(2)}) collective-permute-start(bf16[64,4096]{1,0:T(8,128)(2,1)S(1)} %plus.26), channel_id=1, source_target_pairs={{0,24},{2,26},{4,28},{6,30},{8,0},{10,2},{12,4},{14,6},{16,8},{18,... | collective-permute-start | bytes 1572872 | tf_op jit(solution)/shard_map/back_3_left_0_1/ppermute | solution.py:41
  287.1 20.5 %collective-permute-start.50 = (bf16[128,4096]{1,0:T(8,128)(2,1)S(1)}, bf16[128,4096]{1,0:T(8,128)(2,1)S(1)}, u32[]{:S(2)}, u32[]{:S(2)}) collective-permute-start(bf16[128,4096]{1,0:T(8,128)(2,1)S(1)} %get-tuple-element.83), channel_id=1, source_target_pairs={{0,24},{2,26},{4,28},{6,30},{8,0},{10,2},{12,4},{14,6},{16,8},{18,... | collective-permute-start | bytes 3145736 | tf_op jit(solution)/shard_map/back_1_both_1_1/ppermute | solution.py:41
  289.4 11.0 %collective-permute-start.47 = (bf16[64,4096]{1,0:T(8,128)(2,1)S(1)}, bf16[64,4096]{1,0:T(8,128)(2,1)S(1)}, u32[]{:S(2)}, u32[]{:S(2)}) collective-permute-start(bf16[64,4096]{1,0:T(8,128)(2,1)S(1)} %get-tuple-element.81), channel_id=1, source_target_pairs={{0,8},{2,10},{4,12},{6,14},{8,16},{10,18},{12,20},{14,22},{16,24},... | collective-permute-start | bytes 1572872 | tf_op jit(solution)/shard_map/back_1_far_1_1/ppermute | solution.py:41
  300.5 12.1 %collective-permute-start.48 = (bf16[64,4096]{1,0:T(8,128)(2,1)S(1)}, bf16[64,4096]{1,0:T(8,128)(2,1)S(1)}, u32[]{:S(2)}, u32[]{:S(2)}) collective-permute-start(bf16[64,4096]{1,0:T(8,128)(2,1)S(1)} %plus.28), channel_id=1, source_target_pairs={{0,4},{2,6},{4,0},{6,2},{8,12},{10,14},{12,8},{14,10},{16,20},{18,... | collective-permute-start | bytes 1572872 | tf_op jit(solution)/shard_map/back_2_1_1/ppermute | solution.py:41
  307.7 10.8 %collective-permute-start.52 = (bf16[64,4096]{1,0:T(8,128)(2,1)S(1)}, bf16[64,4096]{1,0:T(8,128)(2,1)S(1)}, u32[]{:S(2)}, u32[]{:S(2)}) collective-permute-start(bf16[64,4096]{1,0:T(8,128)(2,1)S(1)} %plus.31), channel_id=1, source_target_pairs={{0,4},{2,6},{4,0},{6,2},{8,12},{10,14},{12,8},{14,10},{16,20},{18,... | collective-permute-start | bytes 1572872 | tf_op jit(solution)/shard_map/back_3_across_1_1/ppermute | solution.py:41
  312.8 10.5 %collective-permute-start.49 = (bf16[64,4096]{1,0:T(8,128)(2,1)S(1)}, bf16[64,4096]{1,0:T(8,128)(2,1)S(1)}, u32[]{:S(2)}, u32[]{:S(2)}) collective-permute-start(bf16[64,4096]{1,0:T(8,128)(2,1)S(1)} %plus.29), channel_id=1, source_target_pairs={{0,8},{2,10},{4,12},{6,14},{8,16},{10,18},{12,20},{14,22},{16,24},... | collective-permute-start | bytes 1572872 | tf_op jit(solution)/shard_map/back_3_right_1_1/ppermute | solution.py:41
  312.8 12.0 %collective-permute-start.44 = (bf16[64,4096]{1,0:T(8,128)(2,1)S(1)}, bf16[64,4096]{1,0:T(8,128)(2,1)S(1)}, u32[]{:S(2)}, u32[]{:S(2)}) collective-permute-start(bf16[64,4096]{1,0:T(8,128)(2,1)S(1)} %finish.6), channel_id=1, source_target_pairs={{0,32},{32,64},{64,96},{96,0},{1,33},{33,65},{65,97},{97,1},{2,34}... | collective-permute-start | bytes 1572872 | tf_op jit(solution)/shard_map/ppermute | solution.py:46
  (14 other events, 150.9 us)
